TPU v7x, 256 devices: a whole 4x4x8 slice. The times are simulated.
256 devices in a mesh: seq: 8 (over y, core), item: 32 (over z, x).
Axes of the slice: x: 4, y: 4, z: 8, core: 2. Of those that a mesh axis runs over, the one named last changes fastest.
Arguments:
- events: float32 [32, 1024, 512], P('item', 'seq'), may hold values from -6 to 6
- w_uvqk: float32 [512, 2048], replicated, may hold values from -0.25 to 0.25
- out_gain: float32 [512], replicated, may hold values from 0.5 to 1.5
- w_out: float32 [512, 512], replicated, may hold values from -0.25 to 0.25
- item_table: float32 [32768, 512], P('item'), may hold values from -0.25 to 0.25
- user_lengths: int32 [32, 4], P('item'), may hold values from 1 to 512, 1024 in all within a row
- neg_ids: int32 [4, 512], replicated, may hold values from 0 to 1023
- panel_owner: int32 [4], replicated, may hold values from 0 to 31
- block_mask: int32 [32, 8], P('item', 'seq'), may hold values from 1 to 65535
- targets: int32 [32, 1024], P('item', 'seq'), may hold values from 0 to 2047
Outputs:
- mean_loss: float32 [], replicated
- event_grad: float32 [32, 1024, 512], P('item', 'seq')
- table_grad: float32 [32768, 512], P('item')
Inputs may be any that keep to these rules, and one draw needn't show every extreme that they name: `user_lengths`: the 4 lengths of a group sum to 1024, the longest is exactly 512. `neg_ids`: rows may repeat within and across panels. `panel_owner`: several panels may have one owner. `block_mask`: bit k of an entry admits negative columns 128 k to 128 k + 127 for the 128 events of that block.
All inputs are finite; a program needn't handle non-finite values.
Results may differ from a plain program's by a relative error of at most 0.0003.
Values sent between devices are 32-bit elements; how exact they have to be, the bound alone decides.
A program may use at most 64 MiB of HBM per device.

v0:
```python
import jax
import jax.numpy as jnp
from jax import lax
from jax.sharding import PartitionSpec as P

H = 16


highest = lax.Precision.HIGHEST
beta_weight = 0.75
epsilon = 1e-05


def broadcast(shard, axis, root):
    mine = lax.axis_index(axis) == root
    return lax.psum(jnp.where(mine, shard, jnp.zeros_like(shard)), axis)


def user_index(lengths, positions):
    user_ends = jnp.cumsum(lengths)
    return jnp.sum((positions[:, None] >= user_ends[None, :]).astype(jnp.int32), axis=1)


def pointwise(query_rows, key_rows, value_rows, query_pos, key_pos, query_user, key_user):
    scores = jnp.einsum("qhd,khd->hqk", query_rows, key_rows, precision=highest)
    allowed = (query_user[:, None] == key_user[None, :]) & (query_pos[:, None] >= key_pos[None, :])
    weights = jax.nn.silu(scores) * allowed[None, :, :].astype(jnp.float32)
    return jnp.einsum("hqk,khd->qhd", weights, value_rows, precision=highest)


def loss_terms(outputs, negatives, mask_words, target_cols):
    logits = jnp.einsum("td,nd->tn", outputs, negatives, precision=highest)
    columns = jnp.arange(negatives.shape[0], dtype=jnp.int32)
    mask_bits = jnp.repeat(mask_words, 128)
    live_cols = jnp.bitwise_and(
        jnp.right_shift(mask_bits[:, None], columns[None, :] // 128), 1
    ).astype(jnp.float32)
    is_target = (columns[None, :] == target_cols[:, None]).astype(jnp.float32)
    neg_weight = live_cols * (1.0 - is_target)
    loss_part = jnp.sum(
        beta_weight * is_target * jax.nn.softplus(-logits) + neg_weight * jax.nn.softplus(logits)
    )
    grad_logits = neg_weight * jax.nn.sigmoid(logits) - beta_weight * is_target * jax.nn.sigmoid(
        -logits
    )
    grad_rows = jnp.dot(grad_logits, negatives, precision=highest)
    panel_part = jnp.einsum("tn,td->nd", grad_logits, outputs, precision=highest)
    return (loss_part, grad_rows, panel_part)


def per_device(
    events,
    w_uvqk,
    out_gain,
    w_out,
    item_table,
    user_lengths,
    neg_ids,
    panel_owner,
    block_mask,
    targets,
):
    rows_in = events[0]
    tok_rows, width = rows_in.shape
    head_size = width // H
    lengths = user_lengths[0]
    projected = jax.nn.silu(jnp.dot(rows_in, w_uvqk, precision=highest))
    gates_u = projected[:, :width]
    packed = projected[:, width:].reshape(tok_rows, 3, H, head_size)
    spread = lax.all_to_all(packed, "seq", split_axis=2, concat_axis=0, tiled=True)
    group_len = spread.shape[0]
    positions = jnp.arange(group_len, dtype=jnp.int32)
    user_ids = user_index(lengths, positions)
    block_rows = 512

    def one_block(first_row):
        query_rows = lax.dynamic_slice_in_dim(spread[:, 1], first_row, block_rows, 0)
        query_pos = first_row + jnp.arange(block_rows, dtype=jnp.int32)
        query_user = lax.dynamic_slice_in_dim(user_ids, first_row, block_rows, 0)
        return pointwise(
            query_rows, spread[:, 2], spread[:, 0], query_pos, positions, query_user, user_ids
        )

    firsts = jnp.arange(group_len // block_rows, dtype=jnp.int32) * block_rows
    attended = lax.map(one_block, firsts).reshape(group_len, spread.shape[2], head_size)
    attended = lax.all_to_all(attended, "seq", split_axis=0, concat_axis=1, tiled=True)
    attended = attended.reshape(tok_rows, width)
    row_mean = jnp.mean(attended, axis=1, keepdims=True)
    centered = attended - row_mean
    variance = jnp.mean(centered * centered, axis=1, keepdims=True)
    normed = centered * lax.rsqrt(variance + epsilon) * out_gain
    outputs = rows_in + jnp.dot(normed * gates_u, w_out, precision=highest)
    panel_list = []
    for panel_index in range(neg_ids.shape[0]):
        local_rows = item_table[neg_ids[panel_index]]
        panel_list.append(broadcast(local_rows, "item", panel_owner[panel_index]))
    negatives = jnp.concatenate(panel_list, axis=0)
    loss_part, grad_rows, panel_part = loss_terms(outputs, negatives, block_mask[0], targets[0])
    panel_total, loss_total = lax.psum((panel_part, loss_part), ("seq", "item"))
    owned_panels = (panel_owner == lax.axis_index("item")).astype(jnp.float32)
    owned_rows = jnp.repeat(owned_panels, neg_ids.shape[1])
    table_grad = (
        jnp.zeros_like(item_table).at[neg_ids.reshape(-1)].add(panel_total * owned_rows[:, None])
    )
    event_total = tok_rows * lax.axis_size("seq") * lax.axis_size("item")
    return (loss_total / event_total, grad_rows[None], table_grad)


def solution(mesh):
    placed = (
        P("item", "seq", None),
        P(),
        P(),
        P(),
        P("item", None),
        P("item", None),
        P(),
        P(),
        P("item", "seq"),
        P("item", "seq"),
    )
    return jax.shard_map(
        per_device,
        mesh=mesh,
        in_specs=placed,
        out_specs=(P(), P("item", "seq", None), P("item", None)),
        check_vma=False,
    )
```

profile of v0, /device:TPU:1, one launch (start us, length us, event | category | flops | bytes accessed | tf_op | source)
XLA Modules:
  0.0 511.7 jit_solution(2004496451884381589)
XLA Ops:
  7.2 0.0 copy-start
  7.2 4.8 divide_multiply_fusion
  12.0 0.0 copy-start.3
  12.0 1.0 copy-done.3
  13.0 0.9 slice.60
  13.9 1.4 copy.27
  15.3 0.9 copy.28
  16.3 7.3 %all-to-all-start = ((f32[128,3,16,32]{0,3,1,2:T(8,128)}), f32[128,3,16,32]{0,3,1,2:T(8,128)}, u32[]{:S(2)}, u32[]{:S(2)}) async-start(f32[128,3,16,32]{0,3,1,2:T(8,128)} %copy.28), calls=%async_computation | async-start | bytes 1572864 | tf_op jit(solution)/shard_map/all_to_all | solution.py:70
  23.6 0.0 all-reduce.6.cloned.1.call-start
  23.6 0.7 fusion.57
  24.3 1.6 gather_fusion
  25.9 2.3 gather_fusion.1
  29.5 2.3 gather_fusion.2
  32.5 2.3 gather_fusion.3
  35.6 1.1 broadcast_select_fusion.3
  36.6 1.1 broadcast_select_fusion.2
  37.7 1.1 broadcast_select_fusion.1
  38.8 1.1 broadcast_select_fusion
  39.9 0.0 all-reduce.6.cloned.1.call-update
  40.0 0.2 reduce-window.8
  40.2 0.1 convert_reduce_fusion
  40.3 2.5 copy.29
  42.7 1.3 all_to_all.27
  44.0 24.4 %while.11 = (s32[]{:T(128)}, f32[2,512,2,32]{1,3,2,0:T(8,128)S(1)}, f32[1024,3,2,32]{0,3,2,1:T(8,128)S(1)}, s32[2]{0:T(128)S(1)}, s32[1024]{0:T(1024)S(1)}, /*index=5*/s32[]{:T(128)}, s32[]{:T(128)}, s32[]{:T(128)}) while((s32[]{:T(128)}, f32[2,512,2,32]{1,3,2,0:T(8,128)S(1)}, f32[1024,3,2,32]{0,3,2,1:T(8,128)S(1)}, ...), condition=%wide.region_3.4_spmd.clone, body=%wide.region_2.3_spmd.clone.sunk | while | flops 812646912 | bytes 13908123 | solution.py:85
  44.0 0.6 dynamic_slice.24
  46.6 3.6 fusion.75
  50.2 0.7 iota_add_fusion.2
  50.8 0.1 dynamic_slice.25
  50.9 0.4 fusion.76
  51.3 4.9 fusion.77
  56.2 0.6 dynamic_slice.24
  58.8 3.6 fusion.75
  62.4 0.7 iota_add_fusion.2
  63.1 0.1 dynamic_slice.25
  63.1 0.4 fusion.76
  63.5 4.9 fusion.77
  68.4 0.8 copy.35
  69.2 0.0 copy-start.9
  69.2 1.8 reshape.354
  71.0 4.8 all-to-all-start.1
  76.4 5.8 %all-to-all-done.1 = f32[8,1,8192]{2,1,0:T(1,128)S(1)} async-done(((f32[8,1,8192]{2,1,0:T(1,128)}), f32[8,1,8192]{2,1,0:T(1,128)S(1)}, u32[]{:S(2)}, u32[]{:S(2)}) %all-to-all-start.1) | async-done | bytes 262176 | tf_op jit(solution)/shard_map/all_to_all | solution.py:86
  82.2 0.5 broadcast.256
  82.8 1.3 reduce.5
  84.0 0.9 reshape.355
  84.9 1.1 copy.37
  86.0 1.0 copy.36
  87.1 1.1 copy.34
  88.2 2.1 reduce_sum.44
  90.2 1.0 fusion.37
  91.3 2.1 convolution_add_fusion
  93.4 109.2 %all-reduce.6.cloned.1.call-done = (f32[512,512]{1,0:T(8,128)}, f32[512,512]{1,0:T(8,128)}, f32[512,512]{1,0:T(8,128)}, f32[512,512]{1,0:T(8,128)}) async-done(((f32[512,512]{1,0:T(8,128)}, f32[512,512]{1,0:T(8,128)}, f32[512,512]{1,0:T(8,128)}, f32[512,512]{1,0:T(8,128)}), (f32[512,512]{1,0:T(8,128)}, f32[512,512]{1,0:T(8,128)}, f32[512,512]{1,0:T(8,128)}, ...) | async-done | bytes 4194320 | tf_op jit(solution)/shard_map/psum | solution.py:16
  202.6 1.4 constant_dynamic-update-slice_fusion.3
  204.0 1.3 constant_dynamic-update-slice_fusion.2
  205.3 0.1 constant_dynamic-update-slice_fusion.1
  205.4 0.1 constant_dynamic-update-slice_fusion
  205.5 2.0 copy-done.6
  207.5 6.1 %fusion.32 = (f32[]{:T(128)}, f32[128,2048]{1,0:T(8,128)S(1)}) fusion(f32[2048]{0:T(1024)S(1)} %fusion.50, s32[128]{0:T(128)S(1)} %bitcast.105, f32[128,512]{1,0:T(8,128)S(1)} %convolution_add_fusion, f32[2048,512]{1,0:T(8,128)S(1)} %constant_dynamic-update-slice_fusion), kind=kOutput, calls=%fused_computation.40 | convolution fusion | flops 1616379904 | bytes 5513732 | tf_op jit(solution)/shard_map/td,nd->tn/dot_general | solution.py:32
  213.6 5.4 %fusion.54 = f32[2048,512]{1,0:T(8,128)} fusion(f32[128,512]{1,0:T(8,128)S(1)} %convolution_add_fusion, f32[128,2048]{1,0:T(8,128)S(1)} %get-tuple-element.71, f32[2048]{0:T(1024)S(1)} %fusion.50, s32[128]{0:T(128)S(1)} %bitcast.106), kind=kOutput, calls=%fused_computation.95 | convolution fusion | flops 1614020608 | bytes 5513728 | tf_op jit(solution)/shard_map/tn,td->nd/dot_general | solution.py:47
  219.0 0.0 all-reduce.4.cloned.1.call-update
  219.1 0.1 broadcast_bitcast_fusion
  219.2 77.8 %psum.46 = f32[]{:T(128)} all-reduce(f32[]{:T(128)} %get-tuple-element.70), channel_id=1, replica_groups=mesh['seq'=8,'item'=32] {'seq','item'}, use_global_device_ids=true, to_apply=%region_12.13 | all-reduce | flops 1 | bytes 8 | tf_op jit(solution)/shard_map/psum | solution.py:99
  297.6 5.9 %convolution_bitcast_fusion = f32[1,128,512]{2,1,0:T(8,128)} fusion(f32[2048,512]{1,0:T(8,128)} %copy-done.6, f32[128,2048]{1,0:T(8,128)S(1)} %get-tuple-element.71, f32[2048]{0:T(1024)S(1)} %fusion.50, s32[128]{0:T(128)S(1)} %bitcast.107), kind=kOutput, calls=%fused_computation.37 | convolution fusion | flops 1614020608 | bytes 5513728 | tf_op jit(solution)/shard_map/dot_general | solution.py:46
  303.5 184.6 %all-reduce.4.cloned.1.call-done = f32[2048,512]{1,0:T(8,128)} async-done(((f32[2048,512]{1,0:T(8,128)}), f32[2048,512]{1,0:T(8,128)}) %all-reduce.4.cloned.1.call-update) | async-done | bytes 4194320 | tf_op jit(solution)/shard_map/psum | solution.py:99
  488.0 15.7 %scatter_custom_fusion = f32[1024,512]{1,0:T(8,128)} fusion(s32[2048]{0:T(1024)S(1)} %bitcast.98, f32[2048,512]{1,0:T(8,128)} %all-reduce.4.cloned.1.call-done, f32[2048]{0:T(1024)S(1)} %bitcast.95, f32[]{:T(128)} %constant.39.clone.1), kind=kCustom, calls=%fused_computation.30 | custom fusion | flops 2097152 | bytes 6299652 | tf_op jit(solution)/shard_map/scatter-add | solution.py:103
  (36 shorter events, 0.2 us)
Async XLA Ops:
  7.2 17.1 %copy-start = (f32[1024,512]{1,0:T(8,128)S(1)}, f32[1024,512]{1,0:T(8,128)}, u32[]{:S(2)}) copy-start(f32[1024,512]{1,0:T(8,128)} %param.16) | copy-start | bytes 6291460
  12.0 1.0 copy-start.3
  13.0 10.6 %copy-start.7 = (s32[4,512]{1,0:T(4,128)S(1)}, s32[4,512]{1,0:T(4,128)}, u32[]{:S(2)}) copy-start(s32[4,512]{1,0:T(4,128)} %param.18) | copy-start | bytes 24580
  13.0 10.6 %copy-start.8 = (s32[4]{0:T(128)S(1)}, s32[4]{0:T(128)}, u32[]{:S(2)}) copy-start(s32[4]{0:T(128)} %param.19) | copy-start | bytes 52
  16.3 24.0 %all-to-all-start = ((f32[128,3,16,32]{0,3,1,2:T(8,128)}), f32[128,3,16,32]{0,3,1,2:T(8,128)}, u32[]{:S(2)}, u32[]{:S(2)}) async-start(f32[128,3,16,32]{0,3,1,2:T(8,128)} %copy.28), calls=%async_computation | async-start | bytes 1572864 | tf_op jit(solution)/shard_map/all_to_all | solution.py:70
  23.6 179.0 %all-reduce.6.cloned.1.call-start = ((), (), s32[]{:S(2)}) async-start(), calls=%async_computation.3 | async-start | bytes 8388608 | tf_op jit(solution)/shard_map/psum | solution.py:16
  35.5 2.2 copy-start.1
  35.5 3.3 copy-start.2
  37.7 2.3 copy-start.10
  69.2 22.1 %copy-start.9 = (f32[512]{0:T(512)S(1)}, f32[512]{0:T(512)}, u32[]{:S(2)}) copy-start(f32[512]{0:T(512)} %param.14) | copy-start | bytes 6148
  71.0 11.3 %all-to-all-start.1 = ((f32[8,1,8192]{2,1,0:T(1,128)}), f32[8,1,8192]{2,1,0:T(1,128)S(1)}, u32[]{:S(2)}, u32[]{:S(2)}) async-start(f32[8,1,8192]{2,1,0:T(1,128)} %reshape.354), calls=%async_computation.1 | async-start | bytes 524288 | tf_op jit(solution)/shard_map/all_to_all | solution.py:86
  75.8 412.3 %all-reduce.4.cloned.1.call-start = ((), (), s32[]{:S(2)}) async-start(), calls=%async_computation.2 | async-start | bytes 8388608 | tf_op jit(solution)/shard_map/psum | solution.py:99
  202.6 2.8 copy-start.5
  202.6 2.8 copy-start.4
  202.6 4.9 copy-start.11
  205.5 2.0 copy-start.6
Sparse Core Ops, SparseCore 0:
  40.1 162.4 all-reduce.5
  219.2 268.8 all-reduce.3
where the time goes:
time: 513 us; the launch traced here: 512 us
  waiting for transfers between devices  300 us (58%)
  blocking collectives  77.8 us (15%)
  matrix products  41.3 us (8%)
  local copies, waits for them, and re-layouts  30.8 us (6%)
  other arithmetic  26.9 us (5%)
  between operations  19.3 us (4%)
  starting transfers between devices  12.1 us (2%)
    psum x1, waiting for transfers between devices, per_device(): panel_total, loss_total = lax.psum((panel_part, loss_part), ('seq', 'item'))  185 us
    psum x1, waiting for transfers between devices, broadcast(): return lax.psum(jnp.where(mine, shard, jnp.zeros_like(shard)), axis)  109 us
    psum x1, blocking collectives, per_device(): panel_total, loss_total = lax.psum((panel_part, loss_part), ('seq', 'item'))  77.8 us
    scatter-add x1, other arithmetic, per_device(): jnp.zeros_like(item_table).at[neg_ids.reshape(-1)]  15.7 us
  transfers between devices with their start and end apart: 4, of which 3 were waited for; matrix products, arithmetic and copies ran while one was open for 11% of the time, Pallas kernels for 0%

commit v1 on v0

v1 whole, which is shorter than its diff:
```python
import functools

import jax
import jax.numpy as jnp
from jax import lax
from jax.experimental import pallas as pl
from jax.experimental.pallas import tpu as pltpu
from jax.sharding import PartitionSpec as P

H = 16
X_RING = 4
beta_weight = 0.75
epsilon = 1e-05
f32, bf16 = jnp.float32, jnp.bfloat16
MESH = pl.DeviceIdType.MESH
VMEM_LIMIT = 60 * 1024 * 1024

VM = pl.BlockSpec(memory_space=pltpu.VMEM)
SM = pl.BlockSpec(memory_space=pltpu.SMEM)
ANY = pl.BlockSpec(memory_space=pl.ANY)
NN = (((1,), (0,)), ((), ()))
NT = (((1,), (1,)), ((), ()))
TN = (((0,), (0,)), ((), ()))


def split(x):
    hi = x.astype(bf16)
    return hi, (x - hi.astype(f32)).astype(bf16)


def mm(a, b, dims=NN):
    return lax.dot_general(a, b, dims, preferred_element_type=f32)


def mm3(a, b, dims=NN):
    (ah, al), (bh, bl) = a, b
    return mm(ah, bh, dims) + (mm(al, bh, dims) + mm(ah, bl, dims))


def sigmoid(x):
    return 0.5 + 0.5 * jnp.tanh(0.5 * x)


class Place:
    def __init__(self, n_seq, n_item):
        self.S, self.I = n_seq, n_item
        self.X = X_RING
        self.Z = n_item // self.X
        self.Y = n_seq // 2
        self.s = lax.axis_index("seq")
        self.i = lax.axis_index("item")
        self.y, self.c = self.s // 2, self.s % 2
        self.z, self.x = self.i // self.X, self.i % self.X

    def at_x(self, x):
        return (self.s, self.z * self.X + x)

    def at_z(self, z):
        return (self.s, z * self.X + self.x)

    def at_y(self, y):
        return (2 * y + self.c, self.i)

    def at_s(self, s):
        return (s, self.i)

    def partner(self):
        return (2 * self.y + 1 - self.c, self.i)


def rdma(src, dst, send, recv, dev):
    return pltpu.make_async_remote_copy(
        src_ref=src, dst_ref=dst, send_sem=send, recv_sem=recv, device_id=dev, device_id_type=MESH
    )


class Ring4:
    def __init__(self, me, dev, part, src, send, recv):
        self.me, self.dev, self.part, self.src = me, dev, part, src
        self.send, self.recv = send, recv
        self.right, self.left = (me + 1) % 4, (me + 3) % 4
        self.opp = (me + 2) % 4

    def _c(self, slot, src, k, h, to):
        return rdma(src, self.part(k, h), self.send.at[slot], self.recv.at[slot], self.dev(to))

    def start(self):
        me = self.me
        self.r = [self._c(h, self.src(h), me, h, self.right) for h in (0, 1)]
        self.l = [self._c(2 + h, self.src(h), me, h, self.left) for h in (0, 1)]
        self.r[0].start()
        self.l[1].start()
        self.r[1].start()
        self.l[0].start()

    def forward_right(self):
        self.r[0].wait_recv()
        self.fr = self._c(4, self.part(self.left, 0), self.left, 0, self.right)
        self.fr.start()

    def forward_left(self):
        self.l[1].wait_recv()
        self.fl = self._c(5, self.part(self.right, 1), self.right, 1, self.left)
        self.fl.start()

    def wait_left(self):
        self.r[1].wait_recv()

    def wait_right(self):
        self.l[0].wait_recv()

    def wait_opp(self):
        self.fr.wait_recv()
        self.fl.wait_recv()

    def wait_sends(self):
        for c in (*self.r, *self.l, self.fr, self.fl):
            c.wait_send()


class CoreSends:
    def __init__(self, dev, send, recv):
        self.dev, self.send, self.recv, self.copies = dev, send, recv, []

    def push(self, src, dst):
        n = len(self.copies)
        c = rdma(src, dst, self.send.at[n], self.recv.at[n], self.dev)
        c.start()
        self.copies.append(c)

    def finish(self):
        for c in self.copies:
            c.wait()


def entry_barrier(devs):
    barrier = pltpu.get_barrier_semaphore()
    for d in devs:
        pl.semaphore_signal(barrier, inc=1, device_id=d, device_id_type=MESH)
    pl.semaphore_wait(barrier, len(devs))


def seq_peers(pc):
    return [pc.at_s((pc.s + d) % pc.S) for d in range(1, pc.S)]


def plane_peers(pc):
    xs = [pc.at_x((pc.x + d) % pc.X) for d in range(1, pc.X)]
    zs = [pc.at_z((pc.z + d) % pc.Z) for d in range(1, pc.Z)]
    return xs + zs


class SeqGather:
    def __init__(self, pc, src, full, send, recv, csend, crecv, lsem):
        half = src.shape[0] // 2
        self.pc, self.full, self.src = pc, full, src
        part = lambda y, h: full.at[2 * y + pc.c, pl.ds(h * half, half)]
        own = lambda h: src.at[pl.ds(h * half, half)]
        self.ring = Ring4(pc.y, pc.at_y, part, own, send, recv)
        self.core = CoreSends(pc.partner(), csend, crecv)
        self.local = pltpu.make_async_copy(src, full.at[pc.s], lsem)

    def blk(self, y):
        return self.full.at[2 * y + self.pc.c]

    def start(self):
        self.ring.start()
        self.core.push(self.src, self.blk(self.pc.y))
        self.local.start()

    def middle(self):
        r = self.ring
        r.forward_right()
        r.forward_left()
        r.wait_left()
        self.core.push(self.blk(r.left), self.blk(r.left))
        r.wait_right()
        self.core.push(self.blk(r.right), self.blk(r.right))

    def finish(self):
        r = self.ring
        r.wait_opp()
        self.core.push(self.blk(r.opp), self.blk(r.opp))
        r.wait_sends()
        self.core.finish()
        self.local.wait()


SEQ_SEMS = [pltpu.SemaphoreType.DMA((6,))] * 2 + [pltpu.SemaphoreType.DMA((4,))] * 2 + [
    pltpu.SemaphoreType.DMA
]


class Reduce:
    def __init__(self, pc, part, full, rx, sx, rz, own, sems):
        self.pc, self.part, self.full = pc, part, full
        self.rx, self.sx, self.rz, self.own = rx, sx, rz, own
        self.xs, self.xr, self.zs, self.zr, self.gs, self.gr = sems[:6]
        self.a1, self.a2, self.b1, self.b2 = sems[6:10], sems[10:12], sems[12:14], sems[14:16]
        self.sems = sems

    def start_x(self):
        pc = self.pc
        self.cx = []
        for d in (2, 1, 3):
            to = (pc.x + d) % pc.X
            c = rdma(
                self.part.at[to], self.rx.at[d - 1], self.xs.at[d - 1], self.xr.at[d - 1], pc.at_x(to)
            )
            c.start()
            self.cx.append(c)

    def start_z(self):
        pc = self.pc
        for c in self.cx:
            c.wait_recv()
        self.sx[...] = (self.part[pc.x] + self.rx[0]) + (self.rx[1] + self.rx[2])
        self.cz = []
        for d in range(1, pc.Z):
            to = (pc.z + d) % pc.Z
            c = rdma(self.sx.at[to], self.rz.at[d - 1], self.zs.at[d - 1], self.zr.at[d - 1], pc.at_z(to))
            c.start()
            self.cz.append(c)

    def start_gather(self):
        pc = self.pc
        total = self.sx[pc.z]
        for d, c in enumerate(self.cz):
            c.wait_recv()
        for d in range(pc.Z - 1):
            total = total + self.rz[d]
        half = total.shape[1] // 2
        rows = total.shape[0]
        self.own[0] = total[:, :half]
        self.own[1] = total[:, half:]
        mine = self.full.at[:, pc.y, pc.c, pc.x, pl.ds(pl.multiple_of(pc.z * rows, rows), rows), :]
        self.local = pltpu.make_async_copy(self.own, mine, self.sems[16])
        self.local.start()
        self.cg = []
        for d in range(1, pc.Z):
            to = (pc.z + d) % pc.Z
            c = rdma(self.own, mine, self.gs.at[d - 1], self.gr.at[d - 1], pc.at_z(to))
            c.start()
            self.cg.append(c)

    def rings(self):
        pc, full, sems = self.pc, self.full, self.sems
        zr = full.shape[4]
        hz = zr // 2
        for c in self.cg:
            c.wait_recv()
        self.local.wait()

        ax_part = lambda k, h: full.at[0, pc.y, pc.c, k, pl.ds(h * hz, hz), :]
        ax = Ring4(pc.x, pc.at_x, ax_part, lambda h: ax_part(pc.x, h), sems[6], sems[7])
        by_part = lambda k, h: full.at[1, k, pc.c, pc.x, pl.ds(h * hz, hz), :]
        by = Ring4(pc.y, pc.at_y, by_part, lambda h: by_part(pc.y, h), sems[8], sems[9])
        ay_part = lambda k, h: full.at[0, k, pc.c, pl.ds(2 * h, 2), :, :]
        ay = Ring4(pc.y, pc.at_y, ay_part, lambda h: ay_part(pc.y, h), sems[10], sems[11])
        bx_part = lambda k, h: full.at[1, pl.ds(2 * h, 2), pc.c, k, :, :]
        bx = Ring4(pc.x, pc.at_x, bx_part, lambda h: bx_part(pc.x, h), sems[12], sems[13])
        core = CoreSends(pc.partner(), sems[14], sems[15])
        a_blk = lambda k: full.at[0, k, pc.c]
        b_blk = lambda k: full.at[1, :, pc.c, k]
        push_a = lambda k: core.push(a_blk(k), a_blk(k))
        push_b = lambda k: core.push(b_blk(k), b_blk(k))

        ax.start()
        by.start()
        ax.forward_right()
        by.forward_right()
        ax.forward_left()
        by.forward_left()
        ax.wait_left()
        ax.wait_right()
        ax.wait_opp()
        ay.start()
        push_a(pc.y)
        by.wait_left()
        by.wait_right()
        by.wait_opp()
        bx.start()
        push_b(pc.x)
        ay.forward_right()
        bx.forward_right()
        ay.forward_left()
        bx.forward_left()
        ay.wait_left()
        push_a(ay.left)
        bx.wait_left()
        push_b(bx.left)
        ay.wait_right()
        push_a(ay.right)
        bx.wait_right()
        push_b(bx.right)
        ay.wait_opp()
        push_a(ay.opp)
        bx.wait_opp()
        push_b(bx.opp)
        for r in (ax, by, ay, bx):
            r.wait_sends()
        for c in (*self.cx, *self.cz, *self.cg):
            c.wait_send()
        core.finish()


def reduce_scratch(X, Z, R, D):
    D6 = pltpu.SemaphoreType.DMA((6,))
    D8 = pltpu.SemaphoreType.DMA((8,))
    DX = pltpu.SemaphoreType.DMA((X - 1,))
    DZ = pltpu.SemaphoreType.DMA((max(Z - 1, 1),))
    return [
        pltpu.VMEM((X - 1, Z, R, D), f32),
        pltpu.VMEM((Z, R, D), f32),
        pltpu.VMEM((max(Z - 1, 1), R, D), f32),
        pltpu.VMEM((2, R, D // 2), f32),
        DX, DX, DZ, DZ, DZ, DZ,
        D6, D6, D6, D6, D6, D6, D6, D6,
        D8, D8,
        pltpu.SemaphoreType.DMA,
    ]


N_REDUCE = 21


def gather_rows_kernel(n_seq, n_item, neg_ref, owner_ref, table_ref, part_ref):
    pc = Place(n_seq, n_item)
    rows, share = table_ref.shape[0], part_ref.shape[0]
    per_panel = neg_ref.shape[1] // share
    panel = pc.s // per_panel
    first = pl.multiple_of((pc.s % per_panel) * share, share)
    ids = neg_ref[pl.ds(panel, 1), pl.ds(first, share)]
    own = owner_ref[panel] == pc.i

    @pl.when(own)
    def _():
        spot = lax.broadcasted_iota(jnp.int32, (rows, share), 0)
        pick = jnp.where(spot == ids, 1.0, 0.0).astype(bf16)
        hi, lo = split(table_ref[...])
        part_ref[...] = mm(pick, hi, TN) + mm(pick, lo, TN)

    @pl.when(jnp.logical_not(own))
    def _():
        part_ref[...] = jnp.zeros_like(part_ref)


def first_kernel(n_seq, n_item, ev_ref, part_ref, ev_all, neg_all, *scratch):
    pc = Place(n_seq, n_item)
    seq = SeqGather(pc, ev_ref.at[0], ev_all, *scratch[:5])
    red = Reduce(pc, part_ref, neg_all, *scratch[5:9], scratch[9:])
    entry_barrier(plane_peers(pc) + seq_peers(pc))
    red.start_x()
    seq.start()
    red.start_z()
    seq.middle()
    red.start_gather()
    seq.finish()
    red.rings()


def attention_kernel(
    n_seq, n_item, ev_all, lens_ref, w_ref, gain_ref, wo_ref, tgt_ref, msk_ref, out_ref,
    xw, xh, xl, kvh, kvl, qs, gates, att, allow, sem,
):
    pc = Place(n_seq, n_item)
    tok, D = xw.shape[1], xw.shape[2]
    win = xw.shape[0] * tok
    w0 = jnp.maximum(pc.s - (xw.shape[0] - 1), 0)
    copy = pltpu.make_async_copy(ev_all.at[pl.ds(w0, xw.shape[0])], xw, sem)
    copy.start()
    copy.wait()
    q_blk = pc.s - w0
    hi, lo = split(xw[...].reshape(win, D))
    xh[...] = hi
    xl[...] = lo
    half = D // 2

    def project(first, xs):
        return mm3(xs, split(w_ref[:, pl.ds(pl.multiple_of(first, half), half)]))

    def kv_step(n, _):
        r = project(jnp.where(n < 2, D + n * half, 2 * D + n * half), (xh[...], xl[...]))
        kvh[n], kvl[n] = split(r * sigmoid(r))
        return 0

    lax.fori_loop(0, 4, kv_step, 0)
    x_own = xw[q_blk]
    xo = split(x_own)
    for n in range(2):
        r = project(2 * D + n * half, xo)
        qs[n] = r * sigmoid(r)
        r = project(n * half, xo)
        gates[n] = r * sigmoid(r)

    row = pc.s * tok + lax.broadcasted_iota(jnp.int32, (tok, win), 0)
    col = w0 * tok + lax.broadcasted_iota(jnp.int32, (tok, win), 1)
    begin = jnp.zeros((tok, win), jnp.int32)
    end = lens_ref[0, 0]
    for u in range(1, lens_ref.shape[1] + 1):
        begin = jnp.where(row >= end, end, begin)
        if u < lens_ref.shape[1]:
            end = end + lens_ref[0, u]
    allow[...] = jnp.where((col >= begin) & (col <= row), 1.0, 0.0)

    hd = D // H
    hpg = 128 // hd
    lane_head = lax.broadcasted_iota(jnp.int32, (tok, 128), 1) // hd

    def heads(m, _):
        for g in range(half // 128):
            lanes = slice(g * 128, (g + 1) * 128)
            kh, kl = kvh[2 + m][:, lanes], kvl[2 + m][:, lanes]
            vh, vl = kvh[m][:, lanes], kvl[m][:, lanes]
            q = qs[m][:, lanes]
            qst = jnp.concatenate([jnp.where(lane_head == h, q, 0.0) for h in range(hpg)], axis=0)
            qh, ql = split(qst)
            sc = mm(jnp.concatenate([qh, ql], axis=1), jnp.concatenate([kh, kh], axis=1), NT)
            sc = sc + mm(qh, kl, NT)
            p = (sc * sigmoid(sc)).reshape(hpg, tok, win) * allow[...][None]
            ph, plo = split(p.reshape(hpg * tok, win))
            o = mm(ph, jnp.concatenate([vh, vl], axis=1))
            o = (o[:, :128] + o[:, 128:]) + mm(plo, vh)
            got = jnp.zeros((tok, 128), f32)
            for h in range(hpg):
                got = got + jnp.where(lane_head == h, o[h * tok:(h + 1) * tok], 0.0)
            att[m, :, lanes] = got
        return 0

    lax.fori_loop(0, 2, heads, 0)
    a = jnp.concatenate([att[0], att[1]], axis=1)
    centered = a - jnp.mean(a, axis=1, keepdims=True)
    var = jnp.mean(centered * centered, axis=1, keepdims=True)
    normed = centered * lax.rsqrt(var + epsilon) * gain_ref[...]
    gated = normed * jnp.concatenate([gates[0], gates[1]], axis=1)
    out_ref[:tok, :] = x_own + mm3(split(gated), split(wo_ref[...]))
    out_ref[tok:, :] = jnp.zeros((out_ref.shape[0] - tok, D), f32)
    out_ref[tok:tok + 1, :tok] = tgt_ref[...].astype(f32)
    out_ref[tok:tok + 1, tok:2 * tok] = jnp.broadcast_to(msk_ref[...], (1, tok)).astype(f32)


def outputs_kernel(n_seq, n_item, out_ref, out_all, *scratch):
    pc = Place(n_seq, n_item)
    seq = SeqGather(pc, out_ref, out_all, *scratch)
    entry_barrier(seq_peers(pc))
    seq.start()
    seq.middle()
    seq.finish()


def loss_core(logits, target, live):
    m = jnp.where(target, -logits, logits)
    w = jnp.where(target, -beta_weight, live)
    e = jnp.exp(-jnp.abs(m))
    sig = jnp.where(m >= 0.0, 1.0, e) / (1.0 + e)
    return w * sig, jnp.abs(w), jnp.maximum(m, 0.0) + jnp.log1p(e)


def loss_kernel(
    n_seq, n_item, out_all, neg_ref, grad_ref, panel_ref, loss_ref, acc, loss_acc,
):
    pc = Place(n_seq, n_item)
    tok, D = grad_ref.shape[1], grad_ref.shape[2]
    half = D // 2
    share = panel_ref.shape[0]
    mine = out_all[pc.s]
    oh = [split(mine[:tok, k * half:(k + 1) * half]) for k in (0, 1)]
    tcol = jnp.transpose(jnp.broadcast_to(mine[tok:tok + 1, :tok], (tok, tok)))
    tcol = jnp.concatenate([tcol, tcol], axis=1).astype(jnp.int32)
    mcol = jnp.broadcast_to(mine[tok:tok + 1, tok:tok + 1], (tok, 2 * tok)).astype(jnp.int32)
    lane = lax.broadcasted_iota(jnp.int32, (tok, 2 * tok), 1)
    acc[...] = jnp.zeros_like(acc)
    loss_acc[...] = jnp.zeros_like(loss_acc)
    step = 2 * tok

    def own_tokens(j, _):
        at = pl.ds(pl.multiple_of(j * step, step), step)
        n0, n1 = split(neg_ref[0, at, :]), split(neg_ref[1, at, :])
        logits = mm3(oh[0], n0, NT) + mm3(oh[1], n1, NT)
        live = (jnp.right_shift(mcol, 2 * j + lane // 128) & 1).astype(f32)
        g, w, sp = loss_core(logits, lane + j * step == tcol, live)
        loss_acc[...] += w * sp
        gs = split(g)
        acc[0] += mm3(gs, n0)
        acc[1] += mm3(gs, n1)
        return 0

    lax.fori_loop(0, neg_ref.shape[1] // step, own_tokens, 0)
    grad_ref[0, :, :half] = acc[0]
    grad_ref[0, :, half:] = acc[1]
    loss_ref[...] = jnp.broadcast_to(jnp.sum(loss_acc[...]), loss_ref.shape)

    at = pl.ds(pl.multiple_of(pc.s * share, share), share)
    m0, m1 = split(neg_ref[0, at, :]), split(neg_ref[1, at, :])
    sub = lax.broadcasted_iota(jnp.int32, (share, 2 * tok), 0)
    panel_ref[...] = jnp.zeros_like(panel_ref)

    def own_columns(b, _):
        pair = [out_all[2 * b], out_all[2 * b + 1]]
        ob = jnp.concatenate([p[:tok] for p in pair], axis=0)
        tg = jnp.concatenate([p[tok:tok + 1, :tok] for p in pair], axis=1).astype(jnp.int32)
        mk = jnp.concatenate([p[tok:tok + 1, tok:2 * tok] for p in pair], axis=1).astype(jnp.int32)
        obh, obl = split(ob)
        k0 = (obh[:, :half], obl[:, :half])
        k1 = (obh[:, half:], obl[:, half:])
        logits = mm3(m0, k0, NT) + mm3(m1, k1, NT)
        column = pc.s * share + sub
        live = (jnp.right_shift(jnp.broadcast_to(mk, column.shape), column // 128) & 1).astype(f32)
        g, _, _ = loss_core(logits, column == jnp.broadcast_to(tg, column.shape), live)
        panel_ref[...] += mm3(split(g), (obh, obl))
        return 0

    lax.fori_loop(0, out_all.shape[0] // 2, own_columns, 0)


def last_kernel(n_seq, n_item, part_ref, loss_ref, panel_all, total_ref, *scratch):
    pc = Place(n_seq, n_item)
    red = Reduce(pc, part_ref, panel_all, *scratch[:4], scratch[4:N_REDUCE])
    (lx, tx, lz, tz, ls, xs, xr, zs, zr, ss, sr) = scratch[N_REDUCE:]
    entry_barrier(plane_peers(pc) + seq_peers(pc))
    red.start_x()
    copies = []
    for d in range(1, pc.X):
        c = rdma(loss_ref, lx.at[d - 1], xs.at[d - 1], xr.at[d - 1], pc.at_x((pc.x + d) % pc.X))
        c.start()
        copies.append(c)
    red.start_z()
    for c in copies:
        c.wait_recv()
    tx[...] = loss_ref[...] + lx[0] + lx[1] + lx[2]
    more = []
    for d in range(1, pc.Z):
        c = rdma(tx, lz.at[d - 1], zs.at[d - 1], zr.at[d - 1], pc.at_z((pc.z + d) % pc.Z))
        c.start()
        more.append(c)
    red.start_gather()
    total = tx[...]
    for c in more:
        c.wait_recv()
    for d in range(pc.Z - 1):
        total = total + lz[d]
    tz[...] = total
    last = []
    for d in range(1, pc.S):
        c = rdma(tz, ls.at[d - 1], ss.at[d - 1], sr.at[d - 1], pc.at_s((pc.s + d) % pc.S))
        c.start()
        last.append(c)
    red.rings()
    for c in last:
        c.wait_recv()
    for d in range(pc.S - 1):
        total = total + ls[d]
    total_ref[...] = total
    for c in (*copies, *more, *last):
        c.wait_send()


def scatter_kernel(n_item, scale, panel_all, neg_ref, owner_ref, total_ref, table_ref, loss_ref, buf, sem):
    item = lax.axis_index("item")
    rows = table_ref.shape[0]
    panel = neg_ref.shape[1]
    half = buf.shape[2]
    table_ref[...] = jnp.zeros_like(table_ref)
    loss_ref[...] = total_ref[...] * scale
    for p in range(neg_ref.shape[0]):

        @pl.when(owner_ref[p] == item)
        def _():
            copy = pltpu.make_async_copy(panel_all.at[:, pl.ds(p * panel, panel), :], buf, sem)
            copy.start()
            spot = lax.broadcasted_iota(jnp.int32, (rows, panel), 0)
            pick = jnp.where(spot == neg_ref[pl.ds(p, 1), :], 1.0, 0.0).astype(bf16)
            copy.wait()
            for k in (0, 1):
                hi, lo = split(buf[k])
                table_ref[:, k * half:(k + 1) * half] += mm(pick, hi) + mm(pick, lo)


def params(cid=None):
    if cid is None:
        return pltpu.CompilerParams(vmem_limit_bytes=VMEM_LIMIT)
    return pltpu.CompilerParams(
        vmem_limit_bytes=VMEM_LIMIT, collective_id=cid, has_side_effects=True
    )


def per_device(
    n_seq, n_item, events, w_uvqk, out_gain, w_out, item_table,
    user_lengths, neg_ids, panel_owner, block_mask, targets,
):
    _, tok, D = events.shape
    X, Z, Y = X_RING, n_item // X_RING, n_seq // 2
    n_neg = neg_ids.shape[0] * neg_ids.shape[1]
    share = n_neg // n_seq
    R = share // n_item
    half = D // 2
    shape = jax.ShapeDtypeStruct

    part = pl.pallas_call(
        functools.partial(gather_rows_kernel, n_seq, n_item),
        out_shape=shape((share, D), f32),
        in_specs=[VM, SM, VM], out_specs=VM, compiler_params=params(), name="gather_rows",
    )(neg_ids, panel_owner, item_table)

    full = shape((2, Y, 2, X, Z * R, half), f32)
    ev_all, neg_all = pl.pallas_call(
        functools.partial(first_kernel, n_seq, n_item),
        out_shape=(shape((n_seq, tok, D), f32), full),
        in_specs=[VM, VM], out_specs=(ANY, ANY),
        scratch_shapes=SEQ_SEMS + reduce_scratch(X, Z, R, D),
        compiler_params=params(1), name="first_exchange",
    )(events, part.reshape(X, Z, R, D))

    blocks = 5
    win = blocks * tok
    aug = tok + 16
    outputs = pl.pallas_call(
        functools.partial(attention_kernel, n_seq, n_item),
        out_shape=shape((aug, D), f32),
        in_specs=[ANY, SM, VM, VM, VM, VM, VM], out_specs=VM,
        scratch_shapes=[
            pltpu.VMEM((blocks, tok, D), f32),
            pltpu.VMEM((win, D), bf16), pltpu.VMEM((win, D), bf16),
            pltpu.VMEM((4, win, half), bf16), pltpu.VMEM((4, win, half), bf16),
            pltpu.VMEM((2, tok, half), f32), pltpu.VMEM((2, tok, half), f32),
            pltpu.VMEM((2, tok, half), f32), pltpu.VMEM((tok, win), f32),
            pltpu.SemaphoreType.DMA,
        ],
        compiler_params=params(), name="attention",
    )(ev_all, user_lengths, w_uvqk, out_gain.reshape(1, D), w_out, targets, block_mask)

    out_all = pl.pallas_call(
        functools.partial(outputs_kernel, n_seq, n_item),
        out_shape=shape((n_seq, aug, D), f32),
        in_specs=[VM], out_specs=ANY, scratch_shapes=SEQ_SEMS,
        compiler_params=params(2), name="gather_outputs",
    )(outputs)

    event_grad, panel, loss = pl.pallas_call(
        functools.partial(loss_kernel, n_seq, n_item),
        out_shape=(shape((1, tok, D), f32), shape((share, D), f32), shape((8, 128), f32)),
        in_specs=[VM, VM], out_specs=(VM, VM, VM),
        scratch_shapes=[pltpu.VMEM((2, tok, half), f32), pltpu.VMEM((tok, 2 * tok), f32)],
        compiler_params=params(), name="loss",
    )(out_all, neg_all.reshape(2, n_neg, half))

    tile = pltpu.VMEM((8, 128), f32)
    dma = pltpu.SemaphoreType.DMA
    nz = max(Z - 1, 1)
    panel_all, total = pl.pallas_call(
        functools.partial(last_kernel, n_seq, n_item),
        out_shape=(full, shape((8, 128), f32)),
        in_specs=[VM, VM], out_specs=(ANY, VM),
        scratch_shapes=reduce_scratch(X, Z, R, D) + [
            pltpu.VMEM((X - 1, 8, 128), f32), tile, pltpu.VMEM((nz, 8, 128), f32), tile,
            pltpu.VMEM((n_seq - 1, 8, 128), f32),
            dma((X - 1,)), dma((X - 1,)), dma((nz,)), dma((nz,)), dma((n_seq - 1,)), dma((n_seq - 1,)),
        ],
        compiler_params=params(3), name="last_exchange",
    )(panel.reshape(X, Z, R, D), loss)

    scale = 1.0 / (tok * n_seq * n_item)
    table_grad, mean_loss = pl.pallas_call(
        functools.partial(scatter_kernel, n_item, scale),
        out_shape=(shape(item_table.shape, f32), shape((8, 128), f32)),
        in_specs=[ANY, VM, SM, VM], out_specs=(VM, VM),
        scratch_shapes=[pltpu.VMEM((2, neg_ids.shape[1], half), f32), pltpu.SemaphoreType.DMA],
        compiler_params=params(), name="scatter",
    )(panel_all.reshape(2, n_neg, half), neg_ids, panel_owner, total)
    return (mean_loss[0, 0], event_grad, table_grad)


def solution(mesh):
    placed = (
        P("item", "seq", None), P(), P(), P(), P("item", None), P("item", None),
        P(), P(), P("item", "seq"), P("item", "seq"),
    )
    body = functools.partial(per_device, mesh.shape["seq"], mesh.shape["item"])
    return jax.shard_map(
        body, mesh=mesh, in_specs=placed,
        out_specs=(P(), P("item", "seq", None), P("item", None)), check_vma=False,
    )
```

time: 513 us -> 155 us (0.30)
  waiting for transfers between devices: 300 us -> 0 us
  Pallas kernels: 0 us -> 153 us
  blocking collectives: 77.8 us -> 0 us
  matrix products: 41.3 us -> 0 us
  local copies, waits for them, and re-layouts: 30.8 us -> 1.19 us
  other arithmetic: 26.9 us -> 0 us
  between operations: 19.3 us -> 1.32 us
  starting transfers between devices: 12.1 us -> 0 us
    psum x2 -> x0, waiting for transfers between devices: 294 us -> none  [the longest x1 185 us: per_device(): panel_total, loss_total = lax.psum((panel_part, loss_part), ('seq', 'item'))]
    pallas_call x0 -> x7, Pallas kernels: none -> 153 us  [the longest x1 52 us: per_device(): pl.pallas_call(functools.partial(first_kernel, n_seq, n_item), out_shape=...]
    psum x1 -> x0, blocking collectives: 77.8 us -> none  [per_device(): panel_total, loss_total = lax.psum((panel_part, loss_part), ('seq', 'item'))]
    dot_general x9 -> x0, matrix products: 41.3 us -> none  [the longest x2 9.72 us: pointwise(): return jnp.einsum('hqk,khd->qhd', weights, value_rows, precision=highest)]
    scatter-add x1 -> x0, other arithmetic: 15.7 us -> none  [per_device(): jnp.zeros_like(item_table).at[neg_ids.reshape(-1)]]
    all_to_all x2 -> x0, starting transfers between devices: 12.1 us -> none  [the longest x1 7.3 us: per_device(): lax.all_to_all(packed, 'seq', split_axis=2, concat_axis=0, tiled=True)]
    gather x4 -> x0, local copies, waits for them, and re-layouts: 8.66 us -> none  [per_device(): local_rows = item_table[neg_ids[panel_index]]]
    unnamed x32 -> x0, local copies, waits for them, and re-layouts: 8.52 us -> none
  transfers between devices with their start and end apart: 4 -> 0, of which waited for: 3 -> 0; matrix products, arithmetic and copies ran while one was open for 11% -> 0% of each run, Pallas kernels for 0% -> 0%
where the time goes in v1:
time: 155 us; the launch traced here: 156 us
  Pallas kernels  153 us (99%)
    pallas_call x1, Pallas kernels, per_device(): pl.pallas_call(functools.partial(first_kernel, n_seq, n_item), out_shape=...  52 us
    pallas_call x1, Pallas kernels, per_device(): pl.pallas_call(functools.partial(last_kernel, n_seq, n_item), out_shape=(...  45.7 us
    pallas_call x1, Pallas kernels, per_device(): pl.pallas_call(functools.partial(outputs_kernel, n_seq, n_item), out_shap...  17.1 us
    pallas_call x1, Pallas kernels, per_device(): pl.pallas_call(functools.partial(loss_kernel, n_seq, n_item), out_shape=(...  15.8 us
    pallas_call x1, Pallas kernels, per_device(): pl.pallas_call(functools.partial(attention_kernel, n_seq, n_item), out_sh...  12.7 us
    pallas_call x1, Pallas kernels, per_device(): pl.pallas_call(functools.partial(scatter_kernel, n_item, scale), out_shap...  7.47 us

profile of v1, /device:TPU:1, one launch (start us, length us, event | category | flops | bytes accessed | tf_op | source)
XLA Modules:
  0.0 155.7 jit_solution(6305816360414364048)
XLA Ops:
  1.3 2.5 %gather_rows.1 = f32[256,512]{1,0:T(8,128)} custom-call(s32[4,512]{1,0:T(4,128)} %neg_ref.3, s32[4]{0:T(128)} %owner_ref.3, f32[1024,512]{1,0:T(8,128)} %table_ref.1), custom_call_target="tpu_custom_call" | custom-call | tf_op jit(solution)/shard_map/gather_rows/pallas_call | solution.py:599
  3.7 52.0 %first_exchange.1 = (f32[8,128,512]{2,1,0:T(8,128)}, f32[2,4,2,4,64,256]{5,4,3,2,1,0:T(8,128)}) custom-call(f32[1,128,512]{2,1,0:T(8,128)} %ev_ref.1, f32[4,8,8,512]{3,2,1,0:T(8,128)} %bitcast.8), custom_call_target="tpu_custom_call" | custom-call | tf_op jit(solution)/shard_map/first_exchange/pallas_call | solution.py:606
  55.8 12.7 %attention.1.out_ref = f32[144,512]{1,0:T(8,128)} custom-call(f32[8,128,512]{2,1,0:T(8,128)} %get-tuple-element.12.ev_all, s32[1,4]{1,0:T(1,128)} %lens_ref.1, f32[512,2048]{1,0:T(8,128)} %w_ref.1, f32[1,512]{1,0:T(1,128)} %bitcast.10, f32[512,512]{1,0:T(8,128)} %wo_ref.1, s32[1,128]{1,0:T(1,128)} %tgt_ref.1, s32[1,1]{1,0:T(1,128)S(6)} %copy.13.msk_ref), custom_call_target="tpu_custom_call" | custom-call | tf_op jit(solution)/shard_map/attention/pallas_call | solution.py:617
  68.4 17.1 %gather_outputs.1.out_all = f32[8,144,512]{2,1,0:T(8,128)} custom-call(f32[144,512]{1,0:T(8,128)} %attention.1.out_ref), custom_call_target="tpu_custom_call" | custom-call | tf_op jit(solution)/shard_map/gather_outputs/pallas_call | solution.py:632
  85.6 15.8 %loss.1 = (f32[1,128,512]{2,1,0:T(8,128)}, f32[256,512]{1,0:T(8,128)}, f32[8,128]{1,0:T(8,128)}) custom-call(f32[8,144,512]{2,1,0:T(8,128)} %gather_outputs.1.out_all, f32[2,2048,256]{2,1,0:T(8,128)} %bitcast.7), custom_call_target="tpu_custom_call" | custom-call | tf_op jit(solution)/shard_map/loss/pallas_call | solution.py:639
  101.4 45.7 %last_exchange.1 = (f32[2,4,2,4,64,256]{5,4,3,2,1,0:T(8,128)}, f32[8,128]{1,0:T(8,128)}) custom-call(f32[4,8,8,512]{3,2,1,0:T(8,128)} %bitcast.9, f32[8,128]{1,0:T(8,128)} %get-tuple-element.15.loss_ref), custom_call_target="tpu_custom_call" | custom-call | tf_op jit(solution)/shard_map/last_exchange/pallas_call | solution.py:650
  147.0 7.5 %scatter.1 = (f32[1024,512]{1,0:T(8,128)}, f32[8,128]{1,0:T(8,128)}) custom-call(f32[2,2048,256]{2,1,0:T(8,128)} %bitcast.6, s32[4,512]{1,0:T(4,128)} %neg_ref.3, s32[4]{0:T(128)} %owner_ref.3, f32[8,128]{1,0:T(8,128)} %get-tuple-element.17.total_ref), custom_call_target="tpu_custom_call" | custom-call | tf_op jit(solution)/shard_map/scatter/pallas_call | solution.py:663
  154.5 1.2 slice.3

commit v2 on v0

v2 whole, which is shorter than its diff:
```python
import functools

import jax
import jax.numpy as jnp
from jax import lax
from jax.experimental import pallas as pl
from jax.experimental.pallas import tpu as pltpu
from jax.sharding import PartitionSpec as P

H = 16
X_RING = 4
beta_weight = 0.75
epsilon = 1e-05
f32, bf16 = jnp.float32, jnp.bfloat16
MESH = pl.DeviceIdType.MESH
VMEM_LIMIT = 60 * 1024 * 1024

VM = pl.BlockSpec(memory_space=pltpu.VMEM)
SM = pl.BlockSpec(memory_space=pltpu.SMEM)
ANY = pl.BlockSpec(memory_space=pl.ANY)
NN = (((1,), (0,)), ((), ()))
NT = (((1,), (1,)), ((), ()))
TN = (((0,), (0,)), ((), ()))


def split(x):
    hi = x.astype(bf16)
    return hi, (x - hi.astype(f32)).astype(bf16)


def mm(a, b, dims=NN):
    return lax.dot_general(a, b, dims, preferred_element_type=f32)


def mm3(a, b, dims=NN):
    (ah, al), (bh, bl) = a, b
    return mm(ah, bh, dims) + (mm(al, bh, dims) + mm(ah, bl, dims))


def sigmoid(x):
    return 0.5 + 0.5 * jnp.tanh(0.5 * x)


class Place:
    def __init__(self, n_seq, n_item):
        self.S, self.I = n_seq, n_item
        self.X = X_RING
        self.Z = n_item // self.X
        self.Y = n_seq // 2
        self.s = lax.axis_index("seq")
        self.i = lax.axis_index("item")
        self.y, self.c = self.s // 2, self.s % 2
        self.z, self.x = self.i // self.X, self.i % self.X

    def at_x(self, x):
        return (self.s, self.z * self.X + x)

    def at_z(self, z):
        return (self.s, z * self.X + self.x)

    def at_y(self, y):
        return (2 * y + self.c, self.i)

    def at_s(self, s):
        return (s, self.i)

    def partner(self):
        return (2 * self.y + 1 - self.c, self.i)


def rdma(src, dst, send, recv, dev):
    return pltpu.make_async_remote_copy(
        src_ref=src, dst_ref=dst, send_sem=send, recv_sem=recv, device_id=dev, device_id_type=MESH
    )


class Ring4:
    def __init__(self, me, dev, part, send, recv, causal=False):
        self.me, self.dev, self.part, self.causal = me, dev, part, causal
        self.send, self.recv = send, recv
        self.right, self.left = (me + 1) % 4, (me + 3) % 4
        self.opp = (me + 2) % 4

    def _c(self, slot, src, k, h, to):
        return rdma(src, self.part(k, h), self.send.at[slot], self.recv.at[slot], self.dev(to))

    def start(self):
        me = self.me
        self.r = [self._c(h, self.part(me, h), me, h, self.right) for h in (0, 1)]
        self.l1 = self._c(3, self.part(me, 1), me, 1, self.left)
        self.r[0].start()
        self.l1.start()
        self.r[1].start()
        self.l = [self.l1]
        if not self.causal:
            self.l.append(self._c(2, self.part(me, 0), me, 0, self.left))
            self.l[1].start()

    def forward_right(self):
        self.r[0].wait_recv()
        self.fr = self._c(4, self.part(self.left, 0), self.left, 0, self.right)
        self.fr.start()

    def forward_left(self):
        self.l1.wait_recv()
        self.fl = self._c(5, self.part(self.right, 1), self.right, 1, self.left)
        self.fl.start()

    def wait_left(self):
        self.r[1].wait_recv()

    def wait_right(self):
        self.l[1].wait_recv()

    def wait_opp(self):
        self.fr.wait_recv()
        self.fl.wait_recv()

    def wait_sends(self):
        for c in (*self.r, *self.l, self.fr, self.fl):
            c.wait_send()


class CoreSends:
    def __init__(self, dev, send, recv):
        self.dev, self.send, self.recv, self.copies = dev, send, recv, []

    def push(self, src, dst):
        n = len(self.copies)
        c = rdma(src, dst, self.send.at[n], self.recv.at[n], self.dev)
        c.start()
        self.copies.append(c)

    def wait_recv(self, n):
        self.copies[n].wait_recv()

    def wait_sends(self):
        for c in self.copies:
            c.wait_send()


def enter(devs):
    barrier = pltpu.get_barrier_semaphore()
    for d in devs:
        pl.semaphore_signal(barrier, inc=1, device_id=d, device_id_type=MESH)
    return lambda: pl.semaphore_wait(barrier, len(devs))


def seq_peers(pc):
    return [pc.at_s((pc.s + d) % pc.S) for d in range(1, pc.S)]


def plane_peers(pc):
    xs = [pc.at_x((pc.x + d) % pc.X) for d in range(1, pc.X)]
    zs = [pc.at_z((pc.z + d) % pc.Z) for d in range(1, pc.Z)]
    return xs + zs


class SeqGather:
    def __init__(self, pc, full, sems, causal=False):
        send, recv, csend, crecv = sems
        half = full.shape[1] // 2
        self.pc, self.full, self.causal = pc, full, causal
        part = lambda y, h: full.at[2 * y + pc.c, pl.ds(h * half, half)]
        self.ring = Ring4(pc.y, pc.at_y, part, send, recv, causal)
        self.core = CoreSends(pc.partner(), csend, crecv)

    def push(self, y):
        blk = self.full.at[2 * y + self.pc.c]
        self.core.push(blk, blk)

    def start(self):
        self.ring.start()
        self.push(self.pc.y)

    def forward(self):
        self.ring.forward_right()
        self.ring.forward_left()

    def near(self):
        r = self.ring
        r.wait_left()
        self.push(r.left)
        if not self.causal:
            r.wait_right()
            self.push(r.right)

    def far(self):
        self.ring.wait_opp()
        self.push(self.ring.opp)

    def pair(self, n):
        self.core.wait_recv(n)

    def wait_sends(self):
        self.ring.wait_sends()
        self.core.wait_sends()


def dma(n):
    return pltpu.SemaphoreType.DMA((n,))


SEQ_SEMS = [dma(6), dma(6), dma(4), dma(4)]


class Reduce:
    def __init__(self, pc, part, full, rx, sx, rz, own, sems):
        self.pc, self.part, self.full = pc, part, full
        self.rx, self.sx, self.rz, self.own = rx, sx, rz, own
        self.xs, self.xr, self.zs, self.zr, self.gs, self.gr = sems[:6]
        self.sems = sems

    def start_x(self):
        pc = self.pc
        self.cx = []
        for d in (2, 1, 3):
            to = (pc.x + d) % pc.X
            c = rdma(
                self.part.at[to], self.rx.at[d - 1], self.xs.at[d - 1], self.xr.at[d - 1], pc.at_x(to)
            )
            c.start()
            self.cx.append(c)

    def start_z(self):
        pc = self.pc
        for c in self.cx:
            c.wait_recv()
        self.sx[...] = (self.part[pc.x] + self.rx[0]) + (self.rx[1] + self.rx[2])
        self.cz = []
        for d in range(1, pc.Z):
            to = (pc.z + d) % pc.Z
            c = rdma(self.sx.at[to], self.rz.at[d - 1], self.zs.at[d - 1], self.zr.at[d - 1], pc.at_z(to))
            c.start()
            self.cz.append(c)

    def start_gather(self):
        pc = self.pc
        total = self.sx[pc.z]
        for d, c in enumerate(self.cz):
            c.wait_recv()
        for d in range(pc.Z - 1):
            total = total + self.rz[d]
        half = total.shape[1] // 2
        rows = total.shape[0]
        self.own[0] = total[:, :half]
        self.own[1] = total[:, half:]
        mine = self.full.at[:, pc.y, pc.c, pc.x, pl.ds(pl.multiple_of(pc.z * rows, rows), rows), :]
        self.local = pltpu.make_async_copy(self.own, mine, self.sems[16])
        self.local.start()
        self.cg = []
        for d in range(1, pc.Z):
            to = (pc.z + d) % pc.Z
            c = rdma(self.own, mine, self.gs.at[d - 1], self.gr.at[d - 1], pc.at_z(to))
            c.start()
            self.cg.append(c)

    def set_rings(self):
        pc, full, sems = self.pc, self.full, self.sems
        hz = full.shape[4] // 2
        hx, hy = pc.X // 2, pc.Y // 2
        ax = lambda k, h: full.at[0, pc.y, pc.c, k, pl.ds(h * hz, hz), :]
        by = lambda k, h: full.at[1, k, pc.c, pc.x, pl.ds(h * hz, hz), :]
        ay = lambda k, h: full.at[0, k, pc.c, pl.ds(hx * h, hx), :, :]
        bx = lambda k, h: full.at[1, pl.ds(hy * h, hy), pc.c, k, :, :]
        self.ax = Ring4(pc.x, pc.at_x, ax, sems[6], sems[7])
        self.by = Ring4(pc.y, pc.at_y, by, sems[8], sems[9])
        self.ay = Ring4(pc.y, pc.at_y, ay, sems[10], sems[11])
        self.bx = Ring4(pc.x, pc.at_x, bx, sems[12], sems[13])
        self.ca = CoreSends(pc.partner(), sems[14], sems[15])
        self.cb = CoreSends(pc.partner(), sems[17], sems[18])

    def push_a(self, k):
        blk = self.full.at[0, k, self.pc.c]
        self.ca.push(blk, blk)

    def push_b(self, k):
        blk = self.full.at[1, :, self.pc.c, k]
        self.cb.push(blk, blk)

    def rings_start(self):
        self.set_rings()
        for c in self.cg:
            c.wait_recv()
        self.local.wait()
        self.ax.start()
        self.by.start()

    def rings_forward(self):
        self.ax.forward_right()
        self.by.forward_right()
        self.ax.forward_left()
        self.by.forward_left()

    def b_start(self):
        self.by.wait_left()
        self.by.wait_right()
        self.by.wait_opp()
        self.bx.start()
        self.push_b(self.pc.x)

    def a_wait(self):
        self.ax.wait_left()
        self.ax.wait_right()
        self.ax.wait_opp()

    def a_start(self):
        self.ay.start()
        self.push_a(self.pc.y)

    def forward(self, r):
        r.forward_right()
        r.forward_left()

    def near(self, r, push):
        r.wait_left()
        push(r.left)
        r.wait_right()
        push(r.right)

    def far(self, r, push):
        r.wait_opp()
        push(r.opp)

    def wait_core(self):
        for c in (self.ca, self.cb):
            for n in range(4):
                c.wait_recv(n)

    def wait_sends(self):
        for r in (self.ax, self.by, self.ay, self.bx):
            r.wait_sends()
        for c in (*self.cx, *self.cz, *self.cg):
            c.wait_send()
        self.ca.wait_sends()
        self.cb.wait_sends()


def reduce_scratch(X, Z, R, D):
    nz = max(Z - 1, 1)
    return [
        pltpu.VMEM((X - 1, Z, R, D), f32),
        pltpu.VMEM((Z, R, D), f32),
        pltpu.VMEM((nz, R, D), f32),
        pltpu.VMEM((2, R, D // 2), f32),
        dma(X - 1), dma(X - 1), dma(nz), dma(nz), dma(nz), dma(nz),
        dma(6), dma(6), dma(6), dma(6), dma(6), dma(6), dma(6), dma(6),
        dma(4), dma(4), pltpu.SemaphoreType.DMA, dma(4), dma(4),
    ]


N_REDUCE = 23


class LossSum:
    def __init__(self, pc, refs):
        self.pc = pc
        (self.t0, self.lx, self.tx, self.lz, self.tz, self.ls,
         self.xs, self.xr, self.zs, self.zr, self.ss, self.sr) = refs
        self.all = []

    def _send(self, src, dst, send, recv, devs):
        out = []
        for d, dev in enumerate(devs):
            c = rdma(src, dst.at[d], send.at[d], recv.at[d], dev)
            c.start()
            out.append(c)
        self.all += out
        return out

    def start_x(self):
        pc = self.pc
        devs = [pc.at_x((pc.x + d) % pc.X) for d in range(1, pc.X)]
        self.c = self._send(self.t0, self.lx, self.xs, self.xr, devs)

    def _sum(self, own, got, n):
        for c in self.c:
            c.wait_recv()
        total = own[...]
        for d in range(n):
            total = total + got[d]
        return total

    def start_z(self):
        pc = self.pc
        self.tx[...] = self._sum(self.t0, self.lx, pc.X - 1)
        devs = [pc.at_z((pc.z + d) % pc.Z) for d in range(1, pc.Z)]
        self.c = self._send(self.tx, self.lz, self.zs, self.zr, devs)

    def start_s(self):
        pc = self.pc
        self.tz[...] = self._sum(self.tx, self.lz, pc.Z - 1)
        self.c = self._send(self.tz, self.ls, self.ss, self.sr, seq_peers(pc))

    def total(self):
        return self._sum(self.tz, self.ls, self.pc.S - 1)

    def wait_sends(self):
        for c in self.all:
            c.wait_send()


def loss_scratch(X, Z, S):
    nz = max(Z - 1, 1)
    tile = lambda *n: pltpu.VMEM((*n, 8, 128), f32)
    return [
        tile(), tile(X - 1), tile(), tile(nz), tile(), tile(S - 1),
        dma(X - 1), dma(X - 1), dma(nz), dma(nz), dma(S - 1), dma(S - 1),
    ]


N_LOSS = 12


def loss_core(logits, target, live):
    m = jnp.where(target, -logits, logits)
    w = jnp.where(target, -beta_weight, live)
    e = jnp.exp(-jnp.abs(m))
    sig = jnp.where(m >= 0.0, 1.0, e) / (1.0 + e)
    return w * sig, jnp.abs(w), jnp.maximum(m, 0.0) + jnp.log1p(e)


def main_kernel(
    n_seq, n_item, ev_ref, w_ref, gain_ref, wo_ref, table_ref, lens_ref, neg_ref, owner_ref,
    msk_ref, tgt_ref, grad_ref, panel_all, total_ref, *scratch,
):
    pc = Place(n_seq, n_item)
    (ev_all, neg_all, out_all, table, w, wo, wh, wl, kvh, kvl, qs, gates, att, part, panel,
     acc, loss_acc, s_ev, s_table, s_w, s_wo) = scratch[:21]
    rest = scratch[21:]
    ev = SeqGather(pc, ev_all, rest[:4], causal=True)
    out = SeqGather(pc, out_all, rest[4:8])
    rest = rest[8:]
    neg = Reduce(pc, part, neg_all, *rest[:4], rest[4:N_REDUCE])
    rest = rest[N_REDUCE:]
    pan = Reduce(pc, panel, panel_all, *rest[:4], rest[4:N_REDUCE])
    loss = LossSum(pc, rest[N_REDUCE:])

    tok, D = grad_ref.shape[1], grad_ref.shape[2]
    half = D // 2
    step = 2 * tok
    rows = table.shape[0]
    X, Z, R = part.shape[0], part.shape[1], part.shape[2]
    share = X * Z * R
    hd = D // H
    hpg = 128 // hd

    ready = enter(plane_peers(pc) + seq_peers(pc))
    c_ev = pltpu.make_async_copy(ev_ref.at[0], ev_all.at[pc.s], s_ev)
    c_table = pltpu.make_async_copy(table_ref, table, s_table)
    c_w = pltpu.make_async_copy(w_ref, w, s_w)
    c_wo = pltpu.make_async_copy(wo_ref, wo, s_wo)
    for c in (c_ev, c_table, c_w, c_wo):
        c.start()

    per_panel = neg_ref.shape[1] // share
    p = pc.s // per_panel
    first = pl.multiple_of((pc.s % per_panel) * share, share)
    ids = neg_ref[pl.ds(p, 1), pl.ds(first, share)] + rows * owner_ref[pl.ds(p, 1), :]
    spot = pc.i * rows + lax.broadcasted_iota(jnp.int32, (rows, share), 0)
    pick = jnp.where(spot == jnp.broadcast_to(ids, spot.shape), 1.0, 0.0).astype(bf16)
    c_table.wait()
    hi, lo = split(table[...])
    part[...] = (mm(pick, hi, TN) + mm(pick, lo, TN)).reshape(part.shape)
    c_ev.wait()
    ready()
    ev.start()
    neg.start_x()

    c_w.wait()

    def split_w(n, _):
        wh[n], wl[n] = split(w[:, pl.ds(pl.multiple_of(n * half, half), half)])
        return 0

    lax.fori_loop(0, 8, split_w, 0)
    x_own = ev_all[pc.s]
    xo = split(x_own)

    def project(xs, n):
        r = mm3(xs, (wh[n], wl[n]))
        return r * sigmoid(r)

    for n in range(2):
        qs[n] = project(xo, 4 + n)
        gates[n] = project(xo, n)
    att[...] = jnp.zeros_like(att)
    ev.forward()

    lane_head = lax.broadcasted_iota(jnp.int32, (tok, 128), 1) // hd
    row = pc.s * tok + lax.broadcasted_iota(jnp.int32, (tok, step), 0)
    lane = lax.broadcasted_iota(jnp.int32, (tok, step), 1)
    begin = jnp.zeros((tok, step), jnp.int32)
    end = jnp.zeros((1, 1), jnp.int32)
    for u in range(lens_ref.shape[1]):
        end = end + lens_ref[0:1, u:u + 1]
        wide = jnp.broadcast_to(end, row.shape)
        begin = jnp.where(row >= wide, wide, begin)

    def attend(y):
        xs = split(jnp.concatenate([ev_all[2 * y], ev_all[2 * y + 1]], axis=0))

        def kv_step(n, _):
            kvh[n], kvl[n] = split(project(xs, jnp.where(n < 2, 2 + n, 4 + n)))
            return 0

        lax.fori_loop(0, 4, kv_step, 0)
        col = y * step + lane
        allow = jnp.where((col >= begin) & (col <= row), 1.0, 0.0)

        def heads(m, _):
            for g in range(half // 128):
                lanes = slice(g * 128, (g + 1) * 128)
                kh, kl = kvh[2 + m][:, lanes], kvl[2 + m][:, lanes]
                vh, vl = kvh[m][:, lanes], kvl[m][:, lanes]
                q = qs[m][:, lanes]
                stack = [jnp.where(lane_head == h, q, 0.0) for h in range(hpg)]
                qh, ql = split(jnp.concatenate(stack, axis=0))
                two = jnp.concatenate([qh, ql], axis=1)
                sc = mm(two, jnp.concatenate([kh, kh], axis=1), NT) + mm(qh, kl, NT)
                pr = (sc * sigmoid(sc)).reshape(hpg, tok, step) * allow[None]
                ph, plo = split(pr.reshape(hpg * tok, step))
                o = mm(ph, jnp.concatenate([vh, vl], axis=1))
                o = (o[:, :128] + o[:, 128:]) + mm(plo, vh)
                got = att[m, :, lanes]
                for h in range(hpg):
                    got = got + jnp.where(lane_head == h, o[h * tok:(h + 1) * tok], 0.0)
                att[m, :, lanes] = got
            return 0

        lax.fori_loop(0, 2, heads, 0)

    ev.pair(0)
    attend(pc.y)
    ev.near()
    neg.start_z()
    ev.far()
    ev.pair(1)
    attend(ev.ring.left)
    neg.start_gather()
    ev.pair(2)
    attend(ev.ring.opp)
    neg.rings_start()

    a = jnp.concatenate([att[0], att[1]], axis=1)
    centered = a - jnp.mean(a, axis=1, keepdims=True)
    var = jnp.mean(centered * centered, axis=1, keepdims=True)
    normed = centered * lax.rsqrt(var + epsilon) * gain_ref[...]
    gated = normed * jnp.concatenate([gates[0], gates[1]], axis=1)
    c_wo.wait()
    o_own = x_own + mm3(split(gated), split(wo[...]))
    pad = out_all.shape[1] - tok
    out_all[pc.s, :tok, :] = o_own
    out_all[pc.s, tok:, :] = jnp.zeros((pad, D), f32)
    out_all[pc.s, tok:tok + 1, :tok] = tgt_ref[...].astype(f32)
    out_all[pc.s, tok:tok + 1, tok:step] = jnp.broadcast_to(msk_ref[...], (1, tok)).astype(f32)
    out.start()
    neg.rings_forward()
    neg.b_start()
    out.forward()
    neg.a_wait()
    neg.forward(neg.bx)
    out.near()
    neg.near(neg.bx, neg.push_b)
    neg.far(neg.bx, neg.push_b)

    m0 = split(neg_all[0, pc.y, pc.c].reshape(share, half))
    m1 = split(neg_all[1, pc.y, pc.c].reshape(share, half))
    column = pc.s * share + lax.broadcasted_iota(jnp.int32, (share, step), 0)
    panel[...] = jnp.zeros_like(panel)
    loss_acc[...] = jnp.zeros_like(loss_acc)

    def own_columns(y):
        pair = [out_all[2 * y], out_all[2 * y + 1]]
        ob = jnp.concatenate([q[:tok] for q in pair], axis=0)
        tg = jnp.concatenate([q[tok:tok + 1, :tok] for q in pair], axis=1).astype(jnp.int32)
        mk = jnp.concatenate([q[tok:tok + 1, tok:step] for q in pair], axis=1).astype(jnp.int32)
        obh, obl = split(ob)
        logits = mm3(m0, (obh[:, :half], obl[:, :half]), NT)
        logits = logits + mm3(m1, (obh[:, half:], obl[:, half:]), NT)
        bits = jnp.right_shift(jnp.broadcast_to(mk, column.shape), column // 128) & 1
        g, wt, sp = loss_core(logits, column == jnp.broadcast_to(tg, column.shape), bits.astype(f32))
        loss_acc[...] += wt * sp
        panel[...] += mm3(split(g), (obh, obl)).reshape(panel.shape)

    out.pair(0)
    own_columns(pc.y)
    out.pair(1)
    own_columns(out.ring.left)
    out.far()
    neg.a_start()
    out.pair(2)
    own_columns(out.ring.right)
    out.pair(3)
    own_columns(out.ring.opp)
    loss.t0[...] = jnp.broadcast_to(jnp.sum(loss_acc[...]), loss.t0.shape)
    pan.start_x()
    loss.start_x()

    neg.forward(neg.ay)
    neg.near(neg.ay, neg.push_a)
    neg.far(neg.ay, neg.push_a)
    mine = out_all[pc.s]
    oh = [split(mine[:tok, k * half:(k + 1) * half]) for k in (0, 1)]
    tcol = jnp.transpose(jnp.broadcast_to(mine[tok:tok + 1, :tok], (tok, tok)))
    tcol = jnp.concatenate([tcol, tcol], axis=1).astype(jnp.int32)
    mcol = jnp.broadcast_to(mine[tok:tok + 1, tok:tok + 1], (tok, step)).astype(jnp.int32)
    acc[...] = jnp.zeros_like(acc)

    def own_tokens(j, _):
        n0 = split(neg_all[0, j // 2, j % 2].reshape(share, half))
        n1 = split(neg_all[1, j // 2, j % 2].reshape(share, half))
        logits = mm3(oh[0], n0, NT) + mm3(oh[1], n1, NT)
        live = (jnp.right_shift(mcol, 2 * j + lane // 128) & 1).astype(f32)
        g, _, _ = loss_core(logits, lane + j * share == tcol, live)
        gs = split(g)
        acc[0] += mm3(gs, n0)
        acc[1] += mm3(gs, n1)
        return 0

    pan.start_z()
    loss.start_z()
    neg.wait_core()
    lax.fori_loop(0, 3, own_tokens, 0)
    pan.start_gather()
    loss.start_s()
    lax.fori_loop(3, 7, own_tokens, 0)
    pan.rings_start()
    lax.fori_loop(7, 8, own_tokens, 0)
    grad_ref[0, :, :half] = acc[0]
    grad_ref[0, :, half:] = acc[1]
    pan.rings_forward()
    pan.a_wait()
    pan.a_start()
    pan.b_start()
    pan.forward(pan.ay)
    pan.forward(pan.bx)
    pan.near(pan.ay, pan.push_a)
    pan.near(pan.bx, pan.push_b)
    total_ref[...] = loss.total()
    pan.far(pan.ay, pan.push_a)
    pan.far(pan.bx, pan.push_b)
    pan.wait_core()
    for q in (ev, out, neg, pan, loss):
        q.wait_sends()


def scatter_kernel(n_item, scale, panel_all, neg_ref, owner_ref, total_ref, table_ref, loss_ref, buf, sem):
    item = lax.axis_index("item")
    rows = table_ref.shape[0]
    panel = neg_ref.shape[1]
    half = buf.shape[2]
    table_ref[...] = jnp.zeros_like(table_ref)
    loss_ref[...] = total_ref[...] * scale
    for p in range(neg_ref.shape[0]):

        @pl.when(owner_ref[p] == item)
        def _():
            copy = pltpu.make_async_copy(panel_all.at[:, pl.ds(p * panel, panel), :], buf, sem)
            copy.start()
            spot = lax.broadcasted_iota(jnp.int32, (rows, panel), 0)
            pick = jnp.where(spot == neg_ref[pl.ds(p, 1), :], 1.0, 0.0).astype(bf16)
            copy.wait()
            for k in (0, 1):
                hi, lo = split(buf[k])
                table_ref[:, k * half:(k + 1) * half] += mm(pick, hi) + mm(pick, lo)


def params(cid=None):
    if cid is None:
        return pltpu.CompilerParams(vmem_limit_bytes=VMEM_LIMIT)
    return pltpu.CompilerParams(
        vmem_limit_bytes=VMEM_LIMIT, collective_id=cid, has_side_effects=True
    )


def per_device(
    n_seq, n_item, events, w_uvqk, out_gain, w_out, item_table,
    user_lengths, neg_ids, panel_owner, block_mask, targets,
):
    _, tok, D = events.shape
    X, Z, Y = X_RING, n_item // X_RING, n_seq // 2
    n_neg = neg_ids.shape[0] * neg_ids.shape[1]
    share = n_neg // n_seq
    R = share // n_item
    half = D // 2
    shape = jax.ShapeDtypeStruct

    aug = tok + 16
    step = 2 * tok
    full = (2, Y, 2, X, Z * R, half)
    one = pltpu.SemaphoreType.DMA
    event_grad, panel_all, total = pl.pallas_call(
        functools.partial(main_kernel, n_seq, n_item),
        out_shape=(shape(events.shape, f32), shape(full, f32), shape((8, 128), f32)),
        in_specs=[ANY, ANY, VM, ANY, ANY, VM, VM, VM, VM, VM], out_specs=(VM, ANY, VM),
        scratch_shapes=[
            pltpu.VMEM((n_seq, tok, D), f32), pltpu.VMEM(full, f32),
            pltpu.VMEM((n_seq, aug, D), f32), pltpu.VMEM(item_table.shape, f32),
            pltpu.VMEM(w_uvqk.shape, f32), pltpu.VMEM(w_out.shape, f32),
            pltpu.VMEM((8, D, half), bf16), pltpu.VMEM((8, D, half), bf16),
            pltpu.VMEM((4, step, half), bf16), pltpu.VMEM((4, step, half), bf16),
            pltpu.VMEM((2, tok, half), f32), pltpu.VMEM((2, tok, half), f32),
            pltpu.VMEM((2, tok, half), f32),
            pltpu.VMEM((X, Z, R, D), f32), pltpu.VMEM((X, Z, R, D), f32),
            pltpu.VMEM((2, tok, half), f32), pltpu.VMEM((share, step), f32),
            one, one, one, one,
        ] + SEQ_SEMS * 2 + reduce_scratch(X, Z, R, D) * 2 + loss_scratch(X, Z, n_seq),
        compiler_params=params(1), name="main",
    )(events, w_uvqk, out_gain.reshape(1, D), w_out, item_table, user_lengths, neg_ids,
      panel_owner.reshape(-1, 1), block_mask, targets)

    scale = 1.0 / (tok * n_seq * n_item)
    table_grad, mean_loss = pl.pallas_call(
        functools.partial(scatter_kernel, n_item, scale),
        out_shape=(shape(item_table.shape, f32), shape((8, 128), f32)),
        in_specs=[ANY, VM, SM, VM], out_specs=(VM, VM),
        scratch_shapes=[pltpu.VMEM((2, neg_ids.shape[1], half), f32), pltpu.SemaphoreType.DMA],
        compiler_params=params(), name="scatter",
    )(panel_all.reshape(2, n_neg, half), neg_ids, panel_owner, total)
    return (mean_loss[0, 0], event_grad, table_grad)


def solution(mesh):
    placed = (
        P("item", "seq", None), P(), P(), P(), P("item", None), P("item", None),
        P(), P(), P("item", "seq"), P("item", "seq"),
    )
    body = functools.partial(per_device, mesh.shape["seq"], mesh.shape["item"])
    return jax.shard_map(
        body, mesh=mesh, in_specs=placed,
        out_specs=(P(), P("item", "seq", None), P("item", None)), check_vma=False,
    )
```

time: 513 us -> 111 us (0.22)
  waiting for transfers between devices: 300 us -> 0 us
  Pallas kernels: 0 us -> 106 us
  blocking collectives: 77.8 us -> 0 us
  matrix products: 41.3 us -> 0 us
  local copies, waits for them, and re-layouts: 30.8 us -> 3.22 us
  other arithmetic: 26.9 us -> 0 us
  between operations: 19.3 us -> 1.3 us
  starting transfers between devices: 12.1 us -> 0 us
    psum x2 -> x0, waiting for transfers between devices: 294 us -> none  [the longest x1 185 us: per_device(): panel_total, loss_total = lax.psum((panel_part, loss_part), ('seq', 'item'))]
    pallas_call x0 -> x2, Pallas kernels: none -> 106 us  [the longest x1 101 us: per_device(): pl.pallas_call(functools.partial(main_kernel, n_seq, n_item), out_shape=(...]
    psum x1 -> x0, blocking collectives: 77.8 us -> none  [per_device(): panel_total, loss_total = lax.psum((panel_part, loss_part), ('seq', 'item'))]
    dot_general x9 -> x0, matrix products: 41.3 us -> none  [the longest x2 9.72 us: pointwise(): return jnp.einsum('hqk,khd->qhd', weights, value_rows, precision=highest)]
    scatter-add x1 -> x0, other arithmetic: 15.7 us -> none  [per_device(): jnp.zeros_like(item_table).at[neg_ids.reshape(-1)]]
    all_to_all x2 -> x0, starting transfers between devices: 12.1 us -> none  [the longest x1 7.3 us: per_device(): lax.all_to_all(packed, 'seq', split_axis=2, concat_axis=0, tiled=True)]
    gather x4 -> x0, local copies, waits for them, and re-layouts: 8.66 us -> none  [per_device(): local_rows = item_table[neg_ids[panel_index]]]
    unnamed x32 -> x3, local copies, waits for them, and re-layouts: 8.52 us -> 0.71 us
  transfers between devices with their start and end apart: 4 -> 0, of which waited for: 3 -> 0; matrix products, arithmetic and copies ran while one was open for 11% -> 0% of each run, Pallas kernels for 0% -> 0%
where the time goes in v2:
time: 111 us
  Pallas kernels  106 us (95%)
  local copies, waits for them, and re-layouts  3.22 us (3%)
  between operations  1.3 us (1%)
    pallas_call x1, Pallas kernels, per_device(): pl.pallas_call(functools.partial(main_kernel, n_seq, n_item), out_shape=(...  101 us
    pallas_call x1, Pallas kernels, per_device(): pl.pallas_call(functools.partial(scatter_kernel, n_item, scale), out_shap...  4.97 us

profile of v2, /device:TPU:1, one launch (start us, length us, event | category | flops | bytes accessed | tf_op | source)
XLA Modules:
  0.0 110.7 jit_solution(14353446402104456392)
XLA Ops:
  1.3 1.3 %copy.13.owner_ref = s32[4,1]{1,0:T(4,128)} copy(s32[4,1]{0,1:T(1,128)} %bitcast.6) | data formatting | bytes 32 | tf_op jit(solution)/shard_map/reshape | solution.py:711
  2.6 101.2 %main.1 = (f32[1,128,512]{2,1,0:T(8,128)}, f32[2,4,2,4,64,256]{5,4,3,2,1,0:T(8,128)}, f32[8,128]{1,0:T(8,128)}) custom-call(f32[1,128,512]{2,1,0:T(8,128)} %ev_ref.1, f32[512,2048]{1,0:T(8,128)} %w_ref.1, f32[1,512]{1,0:T(1,128)} %bitcast.5, f32[512,512]{1,0:T(8,128)} %wo_ref.1, f32[1024,512]{1,0:T(8,128)} %table_ref.1, s32[1,4]{1,0:T(1,128)} %lens_ref.1, ...), custom_call_target="tpu_custom_call" | custom-call | tf_op jit(solution)/shard_map/main/pallas_call | solution.py:693
  103.8 0.0 copy-start
  103.8 5.0 %scatter.1 = (f32[1024,512]{1,0:T(8,128)}, f32[8,128]{1,0:T(8,128)}) custom-call(f32[2,2048,256]{2,1,0:T(8,128)} %bitcast.4, s32[4,512]{1,0:T(4,128)} %neg_ref.3, s32[4]{0:T(128)} %owner_ref.1, f32[8,128]{1,0:T(8,128)} %get-tuple-element.9.total_ref), custom_call_target="tpu_custom_call" | custom-call | tf_op jit(solution)/shard_map/scatter/pallas_call | solution.py:714
  108.8 1.2 %slice.3 = f32[1,1]{1,0:T(1,128)} slice(f32[8,128]{1,0:T(8,128)} %get-tuple-element.10), slice={[0:1], [0:1]} | slice | bytes 8 | tf_op jit(solution)/shard_map/slice | solution.py:721
  110.0 0.0 copy-done
  110.0 0.7 copy.16
Async XLA Ops:
  103.8 6.2 %copy-start = (f32[1,128,512]{2,1,0:T(8,128)S(1)}, f32[1,128,512]{2,1,0:T(8,128)}, u32[]{:S(2)}) copy-start(f32[1,128,512]{2,1,0:T(8,128)} %get-tuple-element.17) | copy-start | bytes 786436

commit v3 on v2

--- a/solution.py
+++ b/solution.py
@@ -106,6 +106,10 @@
         self.fl = self._c(5, self.part(self.right, 1), self.right, 1, self.left)
         self.fl.start()
 
+    def forward(self):
+        self.forward_right()
+        self.forward_left()
+
     def wait_left(self):
         self.r[1].wait_recv()
 
@@ -174,8 +178,7 @@
         self.push(self.pc.y)
 
     def forward(self):
-        self.ring.forward_right()
-        self.ring.forward_left()
+        self.ring.forward()
 
     def near(self):
         r = self.ring
@@ -205,28 +208,44 @@
 
 
 class Reduce:
-    def __init__(self, pc, part, full, rx, sx, rz, own, sems):
+    def __init__(self, pc, part, full, refs):
         self.pc, self.part, self.full = pc, part, full
-        self.rx, self.sx, self.rz, self.own = rx, sx, rz, own
-        self.xs, self.xr, self.zs, self.zr, self.gs, self.gr = sems[:6]
-        self.sems = sems
+        (self.rx, self.mid, self.sx, self.rz, self.own, self.xs, self.xr,
+         self.zs, self.zr, self.gs, self.gr, self.lsem) = refs
+        self.hz = part.shape[1] // 2
+        self.right, self.left = (pc.x + 1) % 4, (pc.x + 3) % 4
+        self.opp = (pc.x + 2) % 4
+
+    def _half(self, k, h):
+        return self.part.at[k, pl.ds(h * self.hz, self.hz)]
+
+    def _x(self, slot, src, to):
+        c = rdma(src, self.rx.at[slot], self.xs.at[slot], self.xr.at[slot], self.pc.at_x(to))
+        c.start()
+        self.cx.append(c)
 
     def start_x(self):
-        pc = self.pc
         self.cx = []
-        for d in (2, 1, 3):
-            to = (pc.x + d) % pc.X
-            c = rdma(
-                self.part.at[to], self.rx.at[d - 1], self.xs.at[d - 1], self.xr.at[d - 1], pc.at_x(to)
-            )
-            c.start()
-            self.cx.append(c)
+        self._x(0, self._half(self.opp, 0), self.right)
+        self._x(1, self._half(self.opp, 1), self.left)
+        self._x(2, self._half(self.right, 1), self.right)
+        self._x(3, self._half(self.left, 0), self.left)
+
+    def pass_x(self):
+        h = self.hz
+        self.cx[0].wait_recv()
+        self.mid[0] = self.part[self.right, :h] + self.rx[0]
+        self._x(4, self.mid.at[0], self.right)
+        self.cx[1].wait_recv()
+        self.mid[1] = self.part[self.left, h:] + self.rx[1]
+        self._x(5, self.mid.at[1], self.left)
 
     def start_z(self):
-        pc = self.pc
-        for c in self.cx:
+        pc, h = self.pc, self.hz
+        for c in self.cx[2:]:
             c.wait_recv()
-        self.sx[...] = (self.part[pc.x] + self.rx[0]) + (self.rx[1] + self.rx[2])
+        self.sx[:h] = self.part[pc.x, :h] + (self.rx[4] + self.rx[3])
+        self.sx[h:] = self.part[pc.x, h:] + (self.rx[2] + self.rx[5])
         self.cz = []
         for d in range(1, pc.Z):
             to = (pc.z + d) % pc.Z
@@ -237,7 +256,7 @@
     def start_gather(self):
         pc = self.pc
         total = self.sx[pc.z]
-        for d, c in enumerate(self.cz):
+        for c in self.cz:
             c.wait_recv()
         for d in range(pc.Z - 1):
             total = total + self.rz[d]
@@ -246,7 +265,7 @@
         self.own[0] = total[:, :half]
         self.own[1] = total[:, half:]
         mine = self.full.at[:, pc.y, pc.c, pc.x, pl.ds(pl.multiple_of(pc.z * rows, rows), rows), :]
-        self.local = pltpu.make_async_copy(self.own, mine, self.sems[16])
+        self.local = pltpu.make_async_copy(self.own, mine, self.lsem)
         self.local.start()
         self.cg = []
         for d in range(1, pc.Z):
@@ -255,101 +274,137 @@
             c.start()
             self.cg.append(c)
 
-    def set_rings(self):
-        pc, full, sems = self.pc, self.full, self.sems
-        hz = full.shape[4] // 2
-        hx, hy = pc.X // 2, pc.Y // 2
-        ax = lambda k, h: full.at[0, pc.y, pc.c, k, pl.ds(h * hz, hz), :]
-        by = lambda k, h: full.at[1, k, pc.c, pc.x, pl.ds(h * hz, hz), :]
-        ay = lambda k, h: full.at[0, k, pc.c, pl.ds(hx * h, hx), :, :]
-        bx = lambda k, h: full.at[1, pl.ds(hy * h, hy), pc.c, k, :, :]
-        self.ax = Ring4(pc.x, pc.at_x, ax, sems[6], sems[7])
-        self.by = Ring4(pc.y, pc.at_y, by, sems[8], sems[9])
-        self.ay = Ring4(pc.y, pc.at_y, ay, sems[10], sems[11])
-        self.bx = Ring4(pc.x, pc.at_x, bx, sems[12], sems[13])
-        self.ca = CoreSends(pc.partner(), sems[14], sems[15])
-        self.cb = CoreSends(pc.partner(), sems[17], sems[18])
-
-    def push_a(self, k):
-        blk = self.full.at[0, k, self.pc.c]
-        self.ca.push(blk, blk)
-
-    def push_b(self, k):
-        blk = self.full.at[1, :, self.pc.c, k]
-        self.cb.push(blk, blk)
-
-    def rings_start(self):
-        self.set_rings()
+    def wait_z(self):
         for c in self.cg:
             c.wait_recv()
         self.local.wait()
-        self.ax.start()
-        self.by.start()
-
-    def rings_forward(self):
-        self.ax.forward_right()
-        self.by.forward_right()
-        self.ax.forward_left()
-        self.by.forward_left()
-
-    def b_start(self):
-        self.by.wait_left()
-        self.by.wait_right()
-        self.by.wait_opp()
-        self.bx.start()
-        self.push_b(self.pc.x)
-
-    def a_wait(self):
-        self.ax.wait_left()
-        self.ax.wait_right()
-        self.ax.wait_opp()
-
-    def a_start(self):
-        self.ay.start()
-        self.push_a(self.pc.y)
-
-    def forward(self, r):
-        r.forward_right()
-        r.forward_left()
-
-    def near(self, r, push):
-        r.wait_left()
-        push(r.left)
-        r.wait_right()
-        push(r.right)
-
-    def far(self, r, push):
-        r.wait_opp()
-        push(r.opp)
-
-    def wait_core(self):
-        for c in (self.ca, self.cb):
-            for n in range(4):
-                c.wait_recv(n)
 
     def wait_sends(self):
-        for r in (self.ax, self.by, self.ay, self.bx):
-            r.wait_sends()
         for c in (*self.cx, *self.cz, *self.cg):
             c.wait_send()
-        self.ca.wait_sends()
-        self.cb.wait_sends()
 
 
 def reduce_scratch(X, Z, R, D):
     nz = max(Z - 1, 1)
     return [
-        pltpu.VMEM((X - 1, Z, R, D), f32),
+        pltpu.VMEM((6, Z // 2, R, D), f32),
+        pltpu.VMEM((2, Z // 2, R, D), f32),
         pltpu.VMEM((Z, R, D), f32),
         pltpu.VMEM((nz, R, D), f32),
         pltpu.VMEM((2, R, D // 2), f32),
-        dma(X - 1), dma(X - 1), dma(nz), dma(nz), dma(nz), dma(nz),
-        dma(6), dma(6), dma(6), dma(6), dma(6), dma(6), dma(6), dma(6),
-        dma(4), dma(4), pltpu.SemaphoreType.DMA, dma(4), dma(4),
+        dma(6), dma(6), dma(nz), dma(nz), dma(nz), dma(nz), pltpu.SemaphoreType.DMA,
     ]
 
 
-N_REDUCE = 23
+N_REDUCE = 12
+
+
+class SpreadXY:
+    def __init__(self, pc, full, sems):
+        xs, xr, ys, yr, cs, cr = sems
+        self.pc, self.full = pc, full
+        self.rx = Ring4(pc.x, pc.at_x, lambda k, h: full.at[h, pc.y, pc.c, k], xs, xr)
+        self.ry = Ring4(pc.y, pc.at_y, lambda k, h: full.at[h, k, pc.c], ys, yr)
+        self.core = CoreSends(pc.partner(), cs, cr)
+
+    def push(self, k):
+        blk = self.full.at[:, k, self.pc.c]
+        self.core.push(blk, blk)
+
+    def x_wait(self):
+        self.rx.wait_left()
+        self.rx.wait_right()
+        self.rx.wait_opp()
+
+    def y_start(self):
+        self.ry.start()
+
+    def near(self):
+        self.ry.wait_left()
+        self.push(self.ry.left)
+        self.ry.wait_right()
+        self.push(self.ry.right)
+
+    def far(self):
+        self.ry.wait_opp()
+        self.push(self.ry.opp)
+
+    def wait_sends(self):
+        for q in (self.rx, self.ry, self.core):
+            q.wait_sends()
+
+
+SPREAD_XY_SEMS = [dma(6), dma(6), dma(6), dma(6), dma(4), dma(4)]
+
+
+class Lane:
+    def __init__(self, pc, first, second, blk, sems):
+        (f, fdev), (g, gdev) = first, second
+        self.f, self.g, self.blk = f, g, blk
+        rows = blk(0, 0).shape[0] // 2
+        part = lambda ref, h: ref.at[pl.ds(h * rows, rows), :]
+        self.one = Ring4(f, fdev, lambda k, h: part(blk(k, g), h), sems[0], sems[1])
+        self.two = []
+        for n, k in enumerate((f, (f + 3) % 4, (f + 1) % 4, (f + 2) % 4)):
+            ring = Ring4(
+                g, gdev, lambda j, h, k=k: part(blk(k, j), h), sems[2 + 2 * n], sems[3 + 2 * n]
+            )
+            ring.piece = k
+            self.two.append(ring)
+        self.core = CoreSends(pc.partner(), sems[10], sems[11])
+
+    def push(self, k, j):
+        self.core.push(self.blk(k, j), self.blk(k, j))
+
+    def begin(self, n):
+        ring = self.two[n]
+        ring.start()
+        self.push(ring.piece, self.g)
+
+    def near(self, n):
+        ring = self.two[n]
+        ring.wait_left()
+        self.push(ring.piece, ring.left)
+        ring.wait_right()
+        self.push(ring.piece, ring.right)
+
+    def far(self, n):
+        ring = self.two[n]
+        ring.wait_opp()
+        self.push(ring.piece, ring.opp)
+
+    def steps(self):
+        one, two = self.one, self.two
+        return [
+            lambda: (one.start(), self.begin(0)),
+            lambda: one.forward(),
+            lambda: (one.wait_left(), self.begin(1)),
+            lambda: (one.wait_right(), self.begin(2)),
+            lambda: two[0].forward(),
+            lambda: (one.wait_opp(), self.begin(3)),
+            lambda: two[1].forward(),
+            lambda: two[2].forward(),
+            lambda: self.near(0),
+            lambda: two[3].forward(),
+            lambda: self.near(1),
+            lambda: self.near(2),
+            lambda: self.far(0),
+            lambda: self.near(3),
+            lambda: self.far(1),
+            lambda: self.far(2),
+            lambda: self.far(3),
+        ]
+
+    def wait_core(self):
+        for n in range(16):
+            self.core.wait_recv(n)
+
+    def wait_sends(self):
+        for q in (self.one, *self.two, self.core):
+            q.wait_sends()
+
+
+LANE_SEMS = [dma(6)] * 10 + [dma(16)] * 2
 
 
 class LossSum:
@@ -431,10 +486,14 @@
     ev = SeqGather(pc, ev_all, rest[:4], causal=True)
     out = SeqGather(pc, out_all, rest[4:8])
     rest = rest[8:]
-    neg = Reduce(pc, part, neg_all, *rest[:4], rest[4:N_REDUCE])
-    rest = rest[N_REDUCE:]
-    pan = Reduce(pc, panel, panel_all, *rest[:4], rest[4:N_REDUCE])
-    loss = LossSum(pc, rest[N_REDUCE:])
+    neg = Reduce(pc, part, neg_all, rest[:N_REDUCE])
+    pan = Reduce(pc, panel, panel_all, rest[N_REDUCE:2 * N_REDUCE])
+    rest = rest[2 * N_REDUCE:]
+    spread = SpreadXY(pc, neg_all, rest[:6])
+    along_x, along_y = (pc.x, pc.at_x), (pc.y, pc.at_y)
+    lane_a = Lane(pc, along_x, along_y, lambda k, j: panel_all.at[0, j, pc.c, k], rest[6:18])
+    lane_b = Lane(pc, along_y, along_x, lambda k, j: panel_all.at[1, k, pc.c, j], rest[18:30])
+    loss = LossSum(pc, rest[30:])
 
     tok, D = grad_ref.shape[1], grad_ref.shape[2]
     half = D // 2
@@ -456,7 +515,9 @@
     per_panel = neg_ref.shape[1] // share
     p = pc.s // per_panel
     first = pl.multiple_of((pc.s % per_panel) * share, share)
-    ids = neg_ref[pl.ds(p, 1), pl.ds(first, share)] + rows * owner_ref[pl.ds(p, 1), :]
+    slot = lax.broadcasted_iota(jnp.int32, owner_ref.shape, 1)
+    owner = jnp.sum(jnp.where(slot == p, owner_ref[...], 0), axis=1, keepdims=True)
+    ids = neg_ref[pl.ds(p, 1), pl.ds(first, share)] + rows * jnp.broadcast_to(owner, (1, share))
     spot = pc.i * rows + lax.broadcasted_iota(jnp.int32, (rows, share), 0)
     pick = jnp.where(spot == jnp.broadcast_to(ids, spot.shape), 1.0, 0.0).astype(bf16)
     c_table.wait()
@@ -485,6 +546,7 @@
         qs[n] = project(xo, 4 + n)
         gates[n] = project(xo, n)
     att[...] = jnp.zeros_like(att)
+    neg.pass_x()
     ev.forward()
 
     lane_head = lax.broadcasted_iota(jnp.int32, (tok, 128), 1) // hd
@@ -540,7 +602,8 @@
     neg.start_gather()
     ev.pair(2)
     attend(ev.ring.opp)
-    neg.rings_start()
+    neg.wait_z()
+    spread.rx.start()
 
     a = jnp.concatenate([att[0], att[1]], axis=1)
     centered = a - jnp.mean(a, axis=1, keepdims=True)
@@ -555,14 +618,10 @@
     out_all[pc.s, tok:tok + 1, :tok] = tgt_ref[...].astype(f32)
     out_all[pc.s, tok:tok + 1, tok:step] = jnp.broadcast_to(msk_ref[...], (1, tok)).astype(f32)
     out.start()
-    neg.rings_forward()
-    neg.b_start()
+    spread.rx.forward()
     out.forward()
-    neg.a_wait()
-    neg.forward(neg.bx)
-    out.near()
-    neg.near(neg.bx, neg.push_b)
-    neg.far(neg.bx, neg.push_b)
+    spread.x_wait()
+    spread.push(pc.y)
 
     m0 = split(neg_all[0, pc.y, pc.c].reshape(share, half))
     m1 = split(neg_all[1, pc.y, pc.c].reshape(share, half))
@@ -585,21 +644,19 @@
 
     out.pair(0)
     own_columns(pc.y)
+    out.near()
     out.pair(1)
     own_columns(out.ring.left)
     out.far()
-    neg.a_start()
+    spread.y_start()
     out.pair(2)
     own_columns(out.ring.right)
     out.pair(3)
     own_columns(out.ring.opp)
+    pan.start_x()
     loss.t0[...] = jnp.broadcast_to(jnp.sum(loss_acc[...]), loss.t0.shape)
-    pan.start_x()
     loss.start_x()
 
-    neg.forward(neg.ay)
-    neg.near(neg.ay, neg.push_a)
-    neg.far(neg.ay, neg.push_a)
     mine = out_all[pc.s]
     oh = [split(mine[:tok, k * half:(k + 1) * half]) for k in (0, 1)]
     tcol = jnp.transpose(jnp.broadcast_to(mine[tok:tok + 1, :tok], (tok, tok)))
@@ -607,7 +664,7 @@
     mcol = jnp.broadcast_to(mine[tok:tok + 1, tok:tok + 1], (tok, step)).astype(jnp.int32)
     acc[...] = jnp.zeros_like(acc)
 
-    def own_tokens(j, _):
+    def own_tokens(j):
         n0 = split(neg_all[0, j // 2, j % 2].reshape(share, half))
         n1 = split(neg_all[1, j // 2, j % 2].reshape(share, half))
         logits = mm3(oh[0], n0, NT) + mm3(oh[1], n1, NT)
@@ -616,32 +673,39 @@
         gs = split(g)
         acc[0] += mm3(gs, n0)
         acc[1] += mm3(gs, n1)
-        return 0
-
+
+    def own_pair(n, y):
+        def one(c, _):
+            own_tokens(2 * y + c)
+            return 0
+
+        spread.core.wait_recv(n)
+        lax.fori_loop(0, 2, one, 0)
+
+    own_pair(0, pc.y)
+    pan.pass_x()
+    spread.ry.forward()
     pan.start_z()
     loss.start_z()
-    neg.wait_core()
-    lax.fori_loop(0, 3, own_tokens, 0)
+    spread.near()
+    own_pair(1, spread.ry.left)
     pan.start_gather()
     loss.start_s()
-    lax.fori_loop(3, 7, own_tokens, 0)
-    pan.rings_start()
-    lax.fori_loop(7, 8, own_tokens, 0)
-    grad_ref[0, :, :half] = acc[0]
-    grad_ref[0, :, half:] = acc[1]
-    pan.rings_forward()
-    pan.a_wait()
-    pan.a_start()
-    pan.b_start()
-    pan.forward(pan.ay)
-    pan.forward(pan.bx)
-    pan.near(pan.ay, pan.push_a)
-    pan.near(pan.bx, pan.push_b)
+    own_pair(2, spread.ry.right)
+    pan.wait_z()
+    steps = list(zip(lane_a.steps(), lane_b.steps()))
+    for n, pair in enumerate(steps):
+        for step_of in pair:
+            step_of()
+        if n == 0:
+            spread.far()
+            own_pair(3, spread.ry.opp)
+            grad_ref[0, :, :half] = acc[0]
+            grad_ref[0, :, half:] = acc[1]
     total_ref[...] = loss.total()
-    pan.far(pan.ay, pan.push_a)
-    pan.far(pan.bx, pan.push_b)
-    pan.wait_core()
-    for q in (ev, out, neg, pan, loss):
+    lane_a.wait_core()
+    lane_b.wait_core()
+    for q in (ev, out, neg, pan, spread, lane_a, lane_b, loss):
         q.wait_sends()
 
 
@@ -651,7 +715,7 @@
     panel = neg_ref.shape[1]
     half = buf.shape[2]
     table_ref[...] = jnp.zeros_like(table_ref)
-    loss_ref[...] = total_ref[...] * scale
+    loss_ref[0, 0] = jnp.max(total_ref[...]) * scale
     for p in range(neg_ref.shape[0]):
 
         @pl.when(owner_ref[p] == item)
@@ -705,20 +769,20 @@
             pltpu.VMEM((X, Z, R, D), f32), pltpu.VMEM((X, Z, R, D), f32),
             pltpu.VMEM((2, tok, half), f32), pltpu.VMEM((share, step), f32),
             one, one, one, one,
-        ] + SEQ_SEMS * 2 + reduce_scratch(X, Z, R, D) * 2 + loss_scratch(X, Z, n_seq),
+        ] + SEQ_SEMS * 2 + reduce_scratch(X, Z, R, D) * 2 + SPREAD_XY_SEMS + LANE_SEMS * 2 + loss_scratch(X, Z, n_seq),
         compiler_params=params(1), name="main",
     )(events, w_uvqk, out_gain.reshape(1, D), w_out, item_table, user_lengths, neg_ids,
-      panel_owner.reshape(-1, 1), block_mask, targets)
+      panel_owner.reshape(1, -1), block_mask, targets)
 
     scale = 1.0 / (tok * n_seq * n_item)
     table_grad, mean_loss = pl.pallas_call(
         functools.partial(scatter_kernel, n_item, scale),
-        out_shape=(shape(item_table.shape, f32), shape((8, 128), f32)),
-        in_specs=[ANY, VM, SM, VM], out_specs=(VM, VM),
+        out_shape=(shape(item_table.shape, f32), shape((1, 1), f32)),
+        in_specs=[ANY, VM, SM, VM], out_specs=(VM, SM),
         scratch_shapes=[pltpu.VMEM((2, neg_ids.shape[1], half), f32), pltpu.SemaphoreType.DMA],
         compiler_params=params(), name="scatter",
     )(panel_all.reshape(2, n_neg, half), neg_ids, panel_owner, total)
-    return (mean_loss[0, 0], event_grad, table_grad)
+    return (mean_loss.reshape(()), event_grad, table_grad)
 
 
 def solution(mesh):

time: 111 us -> 97.4 us (0.88)
  Pallas kernels: 106 us -> 95.2 us
  local copies, waits for them, and re-layouts: 3.22 us -> 0.71 us
    pallas_call x1, Pallas kernels: 101 us -> 90.4 us  [per_device(): pl.pallas_call(functools.partial(main_kernel, n_seq, n_item), out_shape=(...]
    reshape x1 -> x0, local copies, waits for them, and re-layouts: 1.31 us -> none  [per_device(): panel_owner.reshape(-1, 1)]
    slice x1 -> x0, local copies, waits for them, and re-layouts: 1.2 us -> none  [per_device(): return (mean_loss[0, 0], event_grad, table_grad)]
where the time goes in v3:
time: 97.4 us; the launch traced here: 97.2 us
  Pallas kernels  95.2 us (98%)
  between operations  1.31 us (1%)
    pallas_call x1, Pallas kernels, per_device(): pl.pallas_call(functools.partial(main_kernel, n_seq, n_item), out_shape=(...  90.4 us
    pallas_call x1, Pallas kernels, per_device(): pl.pallas_call(functools.partial(scatter_kernel, n_item, scale), out_shap...  4.83 us

profile of v3, /device:TPU:1, one launch (start us, length us, event | category | flops | bytes accessed | tf_op | source)
XLA Modules:
  0.0 97.2 jit_solution(3302158969746421486)
XLA Ops:
  1.3 90.4 %main.1 = (f32[1,128,512]{2,1,0:T(8,128)}, f32[2,4,2,4,64,256]{5,4,3,2,1,0:T(8,128)}, f32[8,128]{1,0:T(8,128)}) custom-call(f32[1,128,512]{2,1,0:T(8,128)} %ev_ref.1, f32[512,2048]{1,0:T(8,128)} %w_ref.1, f32[1,512]{1,0:T(1,128)} %bitcast.6, f32[512,512]{1,0:T(8,128)} %wo_ref.1, f32[1024,512]{1,0:T(8,128)} %table_ref.1, s32[1,4]{1,0:T(1,128)} %lens_ref.1, ...), custom_call_target="tpu_custom_call" | custom-call | tf_op jit(solution)/shard_map/main/pallas_call | solution.py:757
  91.7 0.0 copy-start
  91.7 4.8 %scatter.1 = (f32[1024,512]{1,0:T(8,128)}, f32[1,1]{1,0:T(1,128)}) custom-call(f32[2,2048,256]{2,1,0:T(8,128)} %bitcast.4, s32[4,512]{1,0:T(4,128)} %neg_ref.3, s32[4]{0:T(128)} %owner_ref.1, f32[8,128]{1,0:T(8,128)} %get-tuple-element.9.total_ref), custom_call_target="tpu_custom_call" | custom-call | tf_op jit(solution)/shard_map/scatter/pallas_call | solution.py:778
  96.5 0.0 copy-done
  96.5 0.7 copy.15
Async XLA Ops:
  91.7 4.8 %copy-start = (f32[1,128,512]{2,1,0:T(8,128)S(1)}, f32[1,128,512]{2,1,0:T(8,128)}, u32[]{:S(2)}) copy-start(f32[1,128,512]{2,1,0:T(8,128)} %get-tuple-element.17) | copy-start | bytes 786436

commit v4 on v3

--- a/solution.py
+++ b/solution.py
@@ -20,7 +20,6 @@
 ANY = pl.BlockSpec(memory_space=pl.ANY)
 NN = (((1,), (0,)), ((), ()))
 NT = (((1,), (1,)), ((), ()))
-TN = (((0,), (0,)), ((), ()))
 
 
 def split(x):
@@ -512,20 +511,23 @@
     for c in (c_ev, c_table, c_w, c_wo):
         c.start()
 
+    c_ev.wait()
+    ready()
+    ev.start()
+
     per_panel = neg_ref.shape[1] // share
     p = pc.s // per_panel
     first = pl.multiple_of((pc.s % per_panel) * share, share)
     slot = lax.broadcasted_iota(jnp.int32, owner_ref.shape, 1)
     owner = jnp.sum(jnp.where(slot == p, owner_ref[...], 0), axis=1, keepdims=True)
     ids = neg_ref[pl.ds(p, 1), pl.ds(first, share)] + rows * jnp.broadcast_to(owner, (1, share))
-    spot = pc.i * rows + lax.broadcasted_iota(jnp.int32, (rows, share), 0)
-    pick = jnp.where(spot == jnp.broadcast_to(ids, spot.shape), 1.0, 0.0).astype(bf16)
+    ids = jnp.transpose(jnp.broadcast_to(ids - pc.i * rows, (128, share)).astype(f32))
+    spot = lax.broadcasted_iota(jnp.int32, (share, 128), 1).astype(f32)
+    picks = [jnp.where(ids == spot + float(k), 1.0, 0.0).astype(bf16) for k in range(0, rows, 128)]
+    pick = jnp.concatenate(picks, axis=1)
     c_table.wait()
     hi, lo = split(table[...])
-    part[...] = (mm(pick, hi, TN) + mm(pick, lo, TN)).reshape(part.shape)
-    c_ev.wait()
-    ready()
-    ev.start()
+    part[...] = (mm(pick, hi) + mm(pick, lo)).reshape(part.shape)
     neg.start_x()
 
     c_w.wait()
@@ -647,10 +649,10 @@
     out.near()
     out.pair(1)
     own_columns(out.ring.left)
+    out.pair(2)
+    own_columns(out.ring.right)
     out.far()
     spread.y_start()
-    out.pair(2)
-    own_columns(out.ring.right)
     out.pair(3)
     own_columns(out.ring.opp)
     pan.start_x()
@@ -697,7 +699,7 @@
     for n, pair in enumerate(steps):
         for step_of in pair:
             step_of()
-        if n == 0:
+        if n == 9:
             spread.far()
             own_pair(3, spread.ry.opp)
             grad_ref[0, :, :half] = acc[0]

time: 97.4 us -> 99.5 us (1.022)
  Pallas kernels: 95.2 us -> 97.3 us
    pallas_call x1, Pallas kernels: 90.4 us -> 92.5 us  [per_device(): pl.pallas_call(functools.partial(main_kernel, n_seq, n_item), out_shape=(...]
where the time goes in v4:
time: 99.5 us; the launch traced here: 99.3 us
  Pallas kernels  97.3 us (98%)
  between operations  1.31 us (1%)
    pallas_call x1, Pallas kernels, per_device(): pl.pallas_call(functools.partial(main_kernel, n_seq, n_item), out_shape=(...  92.5 us
    pallas_call x1, Pallas kernels, per_device(): pl.pallas_call(functools.partial(scatter_kernel, n_item, scale), out_shap...  4.83 us

profile of v4, /device:TPU:1, one launch (start us, length us, event | category | flops | bytes accessed | tf_op | source)
XLA Modules:
  0.0 99.3 jit_solution(14819450690918506571)
XLA Ops:
  1.3 92.5 %main.1 = (f32[1,128,512]{2,1,0:T(8,128)}, f32[2,4,2,4,64,256]{5,4,3,2,1,0:T(8,128)}, f32[8,128]{1,0:T(8,128)}) custom-call(f32[1,128,512]{2,1,0:T(8,128)} %ev_ref.1, f32[512,2048]{1,0:T(8,128)} %w_ref.1, f32[1,512]{1,0:T(1,128)} %bitcast.6, f32[512,512]{1,0:T(8,128)} %wo_ref.1, f32[1024,512]{1,0:T(8,128)} %table_ref.1, s32[1,4]{1,0:T(1,128)} %lens_ref.1, ...), custom_call_target="tpu_custom_call" | custom-call | tf_op jit(solution)/shard_map/main/pallas_call | solution.py:759
  93.8 0.0 copy-start
  93.8 4.8 %scatter.1 = (f32[1024,512]{1,0:T(8,128)}, f32[1,1]{1,0:T(1,128)}) custom-call(f32[2,2048,256]{2,1,0:T(8,128)} %bitcast.4, s32[4,512]{1,0:T(4,128)} %neg_ref.3, s32[4]{0:T(128)} %owner_ref.1, f32[8,128]{1,0:T(8,128)} %get-tuple-element.9.total_ref), custom_call_target="tpu_custom_call" | custom-call | tf_op jit(solution)/shard_map/scatter/pallas_call | solution.py:780
  98.6 0.0 copy-done
  98.6 0.7 copy.15
Async XLA Ops:
  93.8 4.8 %copy-start = (f32[1,128,512]{2,1,0:T(8,128)S(1)}, f32[1,128,512]{2,1,0:T(8,128)}, u32[]{:S(2)}) copy-start(f32[1,128,512]{2,1,0:T(8,128)} %get-tuple-element.17) | copy-start | bytes 786436

commit v5 on v4

--- a/solution.py
+++ b/solution.py
@@ -128,9 +128,9 @@
     def __init__(self, dev, send, recv):
         self.dev, self.send, self.recv, self.copies = dev, send, recv, []
 
-    def push(self, src, dst):
+    def push(self, blk):
         n = len(self.copies)
-        c = rdma(src, dst, self.send.at[n], self.recv.at[n], self.dev)
+        c = rdma(blk, blk, self.send.at[n], self.recv.at[n], self.dev)
         c.start()
         self.copies.append(c)
 
@@ -169,8 +169,7 @@
         self.core = CoreSends(pc.partner(), csend, crecv)
 
     def push(self, y):
-        blk = self.full.at[2 * y + self.pc.c]
-        self.core.push(blk, blk)
+        self.core.push(self.full.at[2 * y + self.pc.c])
 
     def start(self):
         self.ring.start()
@@ -298,44 +297,6 @@
 N_REDUCE = 12
 
 
-class SpreadXY:
-    def __init__(self, pc, full, sems):
-        xs, xr, ys, yr, cs, cr = sems
-        self.pc, self.full = pc, full
-        self.rx = Ring4(pc.x, pc.at_x, lambda k, h: full.at[h, pc.y, pc.c, k], xs, xr)
-        self.ry = Ring4(pc.y, pc.at_y, lambda k, h: full.at[h, k, pc.c], ys, yr)
-        self.core = CoreSends(pc.partner(), cs, cr)
-
-    def push(self, k):
-        blk = self.full.at[:, k, self.pc.c]
-        self.core.push(blk, blk)
-
-    def x_wait(self):
-        self.rx.wait_left()
-        self.rx.wait_right()
-        self.rx.wait_opp()
-
-    def y_start(self):
-        self.ry.start()
-
-    def near(self):
-        self.ry.wait_left()
-        self.push(self.ry.left)
-        self.ry.wait_right()
-        self.push(self.ry.right)
-
-    def far(self):
-        self.ry.wait_opp()
-        self.push(self.ry.opp)
-
-    def wait_sends(self):
-        for q in (self.rx, self.ry, self.core):
-            q.wait_sends()
-
-
-SPREAD_XY_SEMS = [dma(6), dma(6), dma(6), dma(6), dma(4), dma(4)]
-
-
 class Lane:
     def __init__(self, pc, first, second, blk, sems):
         (f, fdev), (g, gdev) = first, second
@@ -351,26 +312,29 @@
             ring.piece = k
             self.two.append(ring)
         self.core = CoreSends(pc.partner(), sems[10], sems[11])
-
-    def push(self, k, j):
-        self.core.push(self.blk(k, j), self.blk(k, j))
+        self.at = {}
+
+    def push(self, n, to):
+        self.at[n, to] = len(self.core.copies)
+        self.core.push(self.blk(self.two[n].piece, (self.g + to) % 4))
 
     def begin(self, n):
-        ring = self.two[n]
-        ring.start()
-        self.push(ring.piece, self.g)
+        self.two[n].start()
+        self.push(n, 0)
 
     def near(self, n):
         ring = self.two[n]
         ring.wait_left()
-        self.push(ring.piece, ring.left)
+        self.push(n, 3)
         ring.wait_right()
-        self.push(ring.piece, ring.right)
+        self.push(n, 1)
 
     def far(self, n):
-        ring = self.two[n]
-        ring.wait_opp()
-        self.push(ring.piece, ring.opp)
+        self.two[n].wait_opp()
+        self.push(n, 2)
+
+    def arrived(self, n, to):
+        self.core.wait_recv(self.at[n, to])
 
     def steps(self):
         one, two = self.one, self.two
@@ -488,11 +452,16 @@
     neg = Reduce(pc, part, neg_all, rest[:N_REDUCE])
     pan = Reduce(pc, panel, panel_all, rest[N_REDUCE:2 * N_REDUCE])
     rest = rest[2 * N_REDUCE:]
-    spread = SpreadXY(pc, neg_all, rest[:6])
     along_x, along_y = (pc.x, pc.at_x), (pc.y, pc.at_y)
-    lane_a = Lane(pc, along_x, along_y, lambda k, j: panel_all.at[0, j, pc.c, k], rest[6:18])
-    lane_b = Lane(pc, along_y, along_x, lambda k, j: panel_all.at[1, k, pc.c, j], rest[18:30])
-    loss = LossSum(pc, rest[30:])
+
+    def lanes_of(full, sems):
+        a = Lane(pc, along_x, along_y, lambda k, j: full.at[0, j, pc.c, k], sems[:12])
+        b = Lane(pc, along_y, along_x, lambda k, j: full.at[1, k, pc.c, j], sems[12:])
+        return a, b
+
+    na, nb = lanes_of(neg_all, rest[:24])
+    lane_a, lane_b = lanes_of(panel_all, rest[24:48])
+    loss = LossSum(pc, rest[48:])
 
     tok, D = grad_ref.shape[1], grad_ref.shape[2]
     half = D // 2
@@ -510,10 +479,6 @@
     c_wo = pltpu.make_async_copy(wo_ref, wo, s_wo)
     for c in (c_ev, c_table, c_w, c_wo):
         c.start()
-
-    c_ev.wait()
-    ready()
-    ev.start()
 
     per_panel = neg_ref.shape[1] // share
     p = pc.s // per_panel
@@ -528,6 +493,9 @@
     c_table.wait()
     hi, lo = split(table[...])
     part[...] = (mm(pick, hi) + mm(pick, lo)).reshape(part.shape)
+    c_ev.wait()
+    ready()
+    ev.start()
     neg.start_x()
 
     c_w.wait()
@@ -547,65 +515,102 @@
     for n in range(2):
         qs[n] = project(xo, 4 + n)
         gates[n] = project(xo, n)
-    att[...] = jnp.zeros_like(att)
     neg.pass_x()
-    ev.forward()
 
     lane_head = lax.broadcasted_iota(jnp.int32, (tok, 128), 1) // hd
-    row = pc.s * tok + lax.broadcasted_iota(jnp.int32, (tok, step), 0)
-    lane = lax.broadcasted_iota(jnp.int32, (tok, step), 1)
-    begin = jnp.zeros((tok, step), jnp.int32)
+    sub = lax.broadcasted_iota(jnp.int32, (tok, tok), 0)
+    lane = lax.broadcasted_iota(jnp.int32, (tok, tok), 1)
+    row = pc.s * tok + sub
+    begin = jnp.zeros((tok, tok), jnp.int32)
     end = jnp.zeros((1, 1), jnp.int32)
     for u in range(lens_ref.shape[1]):
         end = end + lens_ref[0:1, u:u + 1]
         wide = jnp.broadcast_to(end, row.shape)
         begin = jnp.where(row >= wide, wide, begin)
 
-    def attend(y):
-        xs = split(jnp.concatenate([ev_all[2 * y], ev_all[2 * y + 1]], axis=0))
-
+    def stacked(m, lanes):
+        q = qs[m][:, lanes]
+        parts = [jnp.where(lane_head == h, q, 0.0) for h in range(hpg)]
+        return split(jnp.concatenate(parts, axis=0))
+
+    def collect(m, lanes, o, base):
+        got = base
+        for h in range(hpg):
+            got = got + jnp.where(lane_head == h, o[h * tok:(h + 1) * tok], 0.0)
+        att[m, :, lanes] = got
+
+    def weigh(sc, allow):
+        pr = (sc * sigmoid(sc)).reshape(hpg, tok, sc.shape[1]) * allow[None]
+        return split(pr.reshape(sc.shape))
+
+    def keys_values(xs, n_rows):
         def kv_step(n, _):
-            kvh[n], kvl[n] = split(project(xs, jnp.where(n < 2, 2 + n, 4 + n)))
+            hi, lo = split(project(xs, jnp.where(n < 2, 2 + n, 4 + n)))
+            kvh[n, :n_rows], kvl[n, :n_rows] = hi, lo
             return 0
 
         lax.fori_loop(0, 4, kv_step, 0)
-        col = y * step + lane
-        allow = jnp.where((col >= begin) & (col <= row), 1.0, 0.0)
+
+    def attend_own():
+        keys_values(xo, tok)
+        allow = jnp.where((lane <= sub) & (pc.s * tok + lane >= begin), 1.0, 0.0)
+
+        def heads(m, _):
+            for g in range(half // 128):
+                lanes = slice(g * 128, (g + 1) * 128)
+                kh, kl = kvh[2 + m, :tok, lanes], kvl[2 + m, :tok, lanes]
+                vh, vl = kvh[m, :tok, lanes], kvl[m, :tok, lanes]
+                both = jnp.concatenate(stacked(m, lanes), axis=1)
+                kk = jnp.concatenate([kh, kh], axis=1)
+                k0 = jnp.concatenate([kl, jnp.zeros_like(kl)], axis=1)
+                sc = mm(both, jnp.concatenate([kk, k0], axis=0), NT)
+                pp = jnp.concatenate(weigh(sc[:, :tok] + sc[:, tok:], allow), axis=1)
+                vv = jnp.concatenate([vh, vl], axis=1)
+                o = mm(pp, jnp.concatenate([vv, vv], axis=0))
+                collect(m, lanes, o[:, :128] + o[:, 128:], jnp.zeros((tok, 128), f32))
+            return 0
+
+        lax.fori_loop(0, 2, heads, 0)
+
+    def attend(back):
+        blocks = [(pc.s + pc.S - back - d) % pc.S for d in (0, 1)]
+        keys_values(split(jnp.concatenate([ev_all[b] for b in blocks], axis=0)), step)
+        cols = [b * tok + lane for b in blocks]
+        allow = [jnp.where((c >= begin) & (c <= row), 1.0, 0.0) for c in cols]
+        allow = jnp.concatenate(allow, axis=1)
 
         def heads(m, _):
             for g in range(half // 128):
                 lanes = slice(g * 128, (g + 1) * 128)
                 kh, kl = kvh[2 + m][:, lanes], kvl[2 + m][:, lanes]
                 vh, vl = kvh[m][:, lanes], kvl[m][:, lanes]
-                q = qs[m][:, lanes]
-                stack = [jnp.where(lane_head == h, q, 0.0) for h in range(hpg)]
-                qh, ql = split(jnp.concatenate(stack, axis=0))
+                qh, ql = stacked(m, lanes)
                 two = jnp.concatenate([qh, ql], axis=1)
                 sc = mm(two, jnp.concatenate([kh, kh], axis=1), NT) + mm(qh, kl, NT)
-                pr = (sc * sigmoid(sc)).reshape(hpg, tok, step) * allow[None]
-                ph, plo = split(pr.reshape(hpg * tok, step))
+                ph, plo = weigh(sc, allow)
                 o = mm(ph, jnp.concatenate([vh, vl], axis=1))
                 o = (o[:, :128] + o[:, 128:]) + mm(plo, vh)
-                got = att[m, :, lanes]
-                for h in range(hpg):
-                    got = got + jnp.where(lane_head == h, o[h * tok:(h + 1) * tok], 0.0)
-                att[m, :, lanes] = got
+                collect(m, lanes, o, att[m, :, lanes])
             return 0
 
         lax.fori_loop(0, 2, heads, 0)
 
-    ev.pair(0)
-    attend(pc.y)
+    ev.forward()
+    attend_own()
     ev.near()
     neg.start_z()
+    ev.pair(0)
+    ev.pair(1)
+    attend(1)
     ev.far()
-    ev.pair(1)
-    attend(ev.ring.left)
     neg.start_gather()
     ev.pair(2)
-    attend(ev.ring.opp)
+    attend(3)
     neg.wait_z()
-    spread.rx.start()
+    nb.one.start()
+    nb.begin(0)
+    na.one.start()
+    na.push(0, 0)
 
     a = jnp.concatenate([att[0], att[1]], axis=1)
     centered = a - jnp.mean(a, axis=1, keepdims=True)
@@ -620,10 +625,24 @@
     out_all[pc.s, tok:tok + 1, :tok] = tgt_ref[...].astype(f32)
     out_all[pc.s, tok:tok + 1, tok:step] = jnp.broadcast_to(msk_ref[...], (1, tok)).astype(f32)
     out.start()
-    spread.rx.forward()
+    na.one.forward()
+    nb.one.forward()
+    nb.two[0].forward()
+    na.one.wait_left()
+    na.push(1, 0)
+    na.one.wait_right()
+    na.push(2, 0)
     out.forward()
-    spread.x_wait()
-    spread.push(pc.y)
+    nb.one.wait_left()
+    nb.begin(1)
+    nb.one.wait_right()
+    nb.begin(2)
+    na.one.wait_opp()
+    na.push(3, 0)
+    nb.near(0)
+    nb.one.wait_opp()
+    nb.begin(3)
+    nb.far(0)
 
     m0 = split(neg_all[0, pc.y, pc.c].reshape(share, half))
     m1 = split(neg_all[1, pc.y, pc.c].reshape(share, half))
@@ -646,13 +665,16 @@
 
     out.pair(0)
     own_columns(pc.y)
+    for n in (1, 2, 3):
+        nb.two[n].forward()
     out.near()
     out.pair(1)
     own_columns(out.ring.left)
     out.pair(2)
     own_columns(out.ring.right)
     out.far()
-    spread.y_start()
+    for n in range(4):
+        na.two[n].start()
     out.pair(3)
     own_columns(out.ring.opp)
     pan.start_x()
@@ -666,48 +688,60 @@
     mcol = jnp.broadcast_to(mine[tok:tok + 1, tok:tok + 1], (tok, step)).astype(jnp.int32)
     acc[...] = jnp.zeros_like(acc)
 
+    lane2 = lax.broadcasted_iota(jnp.int32, (tok, step), 1)
+
     def own_tokens(j):
         n0 = split(neg_all[0, j // 2, j % 2].reshape(share, half))
         n1 = split(neg_all[1, j // 2, j % 2].reshape(share, half))
         logits = mm3(oh[0], n0, NT) + mm3(oh[1], n1, NT)
-        live = (jnp.right_shift(mcol, 2 * j + lane // 128) & 1).astype(f32)
-        g, _, _ = loss_core(logits, lane + j * share == tcol, live)
+        live = (jnp.right_shift(mcol, 2 * j + lane2 // 128) & 1).astype(f32)
+        g, _, _ = loss_core(logits, lane2 + j * share == tcol, live)
         gs = split(g)
         acc[0] += mm3(gs, n0)
         acc[1] += mm3(gs, n1)
 
-    def own_pair(n, y):
+    def own_pair(to):
+        y = (pc.y + to) % pc.Y
+        piece = (0, 2, 3, 1)[to]
+
         def one(c, _):
             own_tokens(2 * y + c)
             return 0
 
-        spread.core.wait_recv(n)
+        for n in range(4):
+            na.arrived(n, to)
+            nb.arrived(piece, n)
         lax.fori_loop(0, 2, one, 0)
 
-    own_pair(0, pc.y)
+    for n in range(4):
+        na.two[n].forward()
+    for n in (1, 2, 3):
+        nb.near(n)
+    own_pair(0)
     pan.pass_x()
-    spread.ry.forward()
+    for n in (1, 2, 3):
+        nb.far(n)
+    for n in range(4):
+        na.near(n)
     pan.start_z()
     loss.start_z()
-    spread.near()
-    own_pair(1, spread.ry.left)
+    own_pair(3)
+    for n in range(4):
+        na.far(n)
+    own_pair(1)
     pan.start_gather()
     loss.start_s()
-    own_pair(2, spread.ry.right)
+    own_pair(2)
+    grad_ref[0, :, :half] = acc[0]
+    grad_ref[0, :, half:] = acc[1]
     pan.wait_z()
-    steps = list(zip(lane_a.steps(), lane_b.steps()))
-    for n, pair in enumerate(steps):
+    for pair in zip(lane_a.steps(), lane_b.steps()):
         for step_of in pair:
             step_of()
-        if n == 9:
-            spread.far()
-            own_pair(3, spread.ry.opp)
-            grad_ref[0, :, :half] = acc[0]
-            grad_ref[0, :, half:] = acc[1]
     total_ref[...] = loss.total()
     lane_a.wait_core()
     lane_b.wait_core()
-    for q in (ev, out, neg, pan, spread, lane_a, lane_b, loss):
+    for q in (ev, out, neg, na, nb, pan, lane_a, lane_b, loss):
         q.wait_sends()
 
 
@@ -771,7 +805,7 @@
             pltpu.VMEM((X, Z, R, D), f32), pltpu.VMEM((X, Z, R, D), f32),
             pltpu.VMEM((2, tok, half), f32), pltpu.VMEM((share, step), f32),
             one, one, one, one,
-        ] + SEQ_SEMS * 2 + reduce_scratch(X, Z, R, D) * 2 + SPREAD_XY_SEMS + LANE_SEMS * 2 + loss_scratch(X, Z, n_seq),
+        ] + SEQ_SEMS * 2 + reduce_scratch(X, Z, R, D) * 2 + LANE_SEMS * 4 + loss_scratch(X, Z, n_seq),
         compiler_params=params(1), name="main",
     )(events, w_uvqk, out_gain.reshape(1, D), w_out, item_table, user_lengths, neg_ids,
       panel_owner.reshape(1, -1), block_mask, targets)

time: 99.5 us -> 107 us (1.075)
  Pallas kernels: 97.3 us -> 105 us
    pallas_call x1, Pallas kernels: 92.5 us -> 100 us  [per_device(): pl.pallas_call(functools.partial(main_kernel, n_seq, n_item), out_shape=(...]
where the time goes in v5:
time: 107 us
  Pallas kernels  105 us (98%)
  between operations  1.31 us (1%)
    pallas_call x1, Pallas kernels, per_device(): pl.pallas_call(functools.partial(main_kernel, n_seq, n_item), out_shape=(...  100 us
    pallas_call x1, Pallas kernels, per_device(): pl.pallas_call(functools.partial(scatter_kernel, n_item, scale), out_shap...  4.84 us

profile of v5, /device:TPU:1, one launch (start us, length us, event | category | flops | bytes accessed | tf_op | source)
XLA Modules:
  0.0 107.3 jit_solution(13305404984291311362)
XLA Ops:
  1.3 100.4 %main.1 = (f32[1,128,512]{2,1,0:T(8,128)}, f32[2,4,2,4,64,256]{5,4,3,2,1,0:T(8,128)}, f32[8,128]{1,0:T(8,128)}) custom-call(f32[1,128,512]{2,1,0:T(8,128)} %ev_ref.1, f32[512,2048]{1,0:T(8,128)} %w_ref.1, f32[1,512]{1,0:T(1,128)} %bitcast.6, f32[512,512]{1,0:T(8,128)} %wo_ref.1, f32[1024,512]{1,0:T(8,128)} %table_ref.1, s32[1,4]{1,0:T(1,128)} %lens_ref.1, ...), custom_call_target="tpu_custom_call" | custom-call | tf_op jit(solution)/shard_map/main/pallas_call | solution.py:793
  101.7 0.0 copy-start
  101.7 4.8 %scatter.1 = (f32[1024,512]{1,0:T(8,128)}, f32[1,1]{1,0:T(1,128)}) custom-call(f32[2,2048,256]{2,1,0:T(8,128)} %bitcast.4, s32[4,512]{1,0:T(4,128)} %neg_ref.3, s32[4]{0:T(128)} %owner_ref.1, f32[8,128]{1,0:T(8,128)} %get-tuple-element.9.total_ref), custom_call_target="tpu_custom_call" | custom-call | tf_op jit(solution)/shard_map/scatter/pallas_call | solution.py:814
  106.6 0.0 copy-done
  106.6 0.7 copy.15
Async XLA Ops:
  101.7 4.9 %copy-start = (f32[1,128,512]{2,1,0:T(8,128)S(1)}, f32[1,128,512]{2,1,0:T(8,128)}, u32[]{:S(2)}) copy-start(f32[1,128,512]{2,1,0:T(8,128)} %get-tuple-element.17) | copy-start | bytes 786436

commit v6 on v5

--- a/solution.py
+++ b/solution.py
@@ -553,6 +553,7 @@
 
     def attend_own():
         keys_values(xo, tok)
+        ev.forward()
         allow = jnp.where((lane <= sub) & (pc.s * tok + lane >= begin), 1.0, 0.0)
 
         def heads(m, _):
@@ -572,9 +573,10 @@
 
         lax.fori_loop(0, 2, heads, 0)
 
-    def attend(back):
+    def attend(back, between):
         blocks = [(pc.s + pc.S - back - d) % pc.S for d in (0, 1)]
         keys_values(split(jnp.concatenate([ev_all[b] for b in blocks], axis=0)), step)
+        between()
         cols = [b * tok + lane for b in blocks]
         allow = [jnp.where((c >= begin) & (c <= row), 1.0, 0.0) for c in cols]
         allow = jnp.concatenate(allow, axis=1)
@@ -595,22 +597,26 @@
 
         lax.fori_loop(0, 2, heads, 0)
 
-    ev.forward()
     attend_own()
+    neg.start_z()
     ev.near()
-    neg.start_z()
     ev.pair(0)
     ev.pair(1)
-    attend(1)
+    attend(1, neg.start_gather)
     ev.far()
-    neg.start_gather()
     ev.pair(2)
-    attend(3)
-    neg.wait_z()
-    nb.one.start()
-    nb.begin(0)
-    na.one.start()
-    na.push(0, 0)
+
+    def spread_start():
+        neg.wait_z()
+        nb.one.start()
+        na.one.start()
+        nb.begin(0)
+        na.push(0, 0)
+
+    attend(3, spread_start)
+    nb.one.forward()
+    na.one.forward()
+    nb.two[0].forward()
 
     a = jnp.concatenate([att[0], att[1]], axis=1)
     centered = a - jnp.mean(a, axis=1, keepdims=True)
@@ -625,24 +631,15 @@
     out_all[pc.s, tok:tok + 1, :tok] = tgt_ref[...].astype(f32)
     out_all[pc.s, tok:tok + 1, tok:step] = jnp.broadcast_to(msk_ref[...], (1, tok)).astype(f32)
     out.start()
-    na.one.forward()
-    nb.one.forward()
-    nb.two[0].forward()
     na.one.wait_left()
     na.push(1, 0)
     na.one.wait_right()
     na.push(2, 0)
-    out.forward()
-    nb.one.wait_left()
-    nb.begin(1)
-    nb.one.wait_right()
-    nb.begin(2)
     na.one.wait_opp()
     na.push(3, 0)
     nb.near(0)
-    nb.one.wait_opp()
-    nb.begin(3)
     nb.far(0)
+    out.forward()
 
     m0 = split(neg_all[0, pc.y, pc.c].reshape(share, half))
     m1 = split(neg_all[1, pc.y, pc.c].reshape(share, half))
@@ -665,11 +662,17 @@
 
     out.pair(0)
     own_columns(pc.y)
-    for n in (1, 2, 3):
-        nb.two[n].forward()
+    nb.one.wait_left()
+    nb.begin(1)
+    nb.one.wait_right()
+    nb.begin(2)
+    nb.one.wait_opp()
+    nb.begin(3)
     out.near()
     out.pair(1)
     own_columns(out.ring.left)
+    for n in (1, 2, 3):
+        nb.two[n].forward()
     out.pair(2)
     own_columns(out.ring.right)
     out.far()
@@ -713,18 +716,18 @@
             nb.arrived(piece, n)
         lax.fori_loop(0, 2, one, 0)
 
+    own_pair(0)
+    pan.pass_x()
     for n in range(4):
         na.two[n].forward()
     for n in (1, 2, 3):
         nb.near(n)
-    own_pair(0)
-    pan.pass_x()
+    pan.start_z()
+    loss.start_z()
     for n in (1, 2, 3):
         nb.far(n)
     for n in range(4):
         na.near(n)
-    pan.start_z()
-    loss.start_z()
     own_pair(3)
     for n in range(4):
         na.far(n)
@@ -749,20 +752,25 @@
     item = lax.axis_index("item")
     rows = table_ref.shape[0]
     panel = neg_ref.shape[1]
-    half = buf.shape[2]
+    half = buf.shape[3]
+    def fetch(p):
+        return pltpu.make_async_copy(
+            panel_all.at[:, pl.ds(p * panel, panel), :], buf.at[p], sem.at[p]
+        )
+
+    for p in range(neg_ref.shape[0]):
+        pl.when(owner_ref[p] == item)(fetch(p).start)
     table_ref[...] = jnp.zeros_like(table_ref)
     loss_ref[0, 0] = jnp.max(total_ref[...]) * scale
     for p in range(neg_ref.shape[0]):
 
         @pl.when(owner_ref[p] == item)
         def _():
-            copy = pltpu.make_async_copy(panel_all.at[:, pl.ds(p * panel, panel), :], buf, sem)
-            copy.start()
             spot = lax.broadcasted_iota(jnp.int32, (rows, panel), 0)
             pick = jnp.where(spot == neg_ref[pl.ds(p, 1), :], 1.0, 0.0).astype(bf16)
-            copy.wait()
+            fetch(p).wait()
             for k in (0, 1):
-                hi, lo = split(buf[k])
+                hi, lo = split(buf[p, k])
                 table_ref[:, k * half:(k + 1) * half] += mm(pick, hi) + mm(pick, lo)
 
 
@@ -815,7 +823,7 @@
         functools.partial(scatter_kernel, n_item, scale),
         out_shape=(shape(item_table.shape, f32), shape((1, 1), f32)),
         in_specs=[ANY, VM, SM, VM], out_specs=(VM, SM),
-        scratch_shapes=[pltpu.VMEM((2, neg_ids.shape[1], half), f32), pltpu.SemaphoreType.DMA],
+        scratch_shapes=[pltpu.VMEM((neg_ids.shape[0], 2, neg_ids.shape[1], half), f32), dma(neg_ids.shape[0])],
         compiler_params=params(), name="scatter",
     )(panel_all.reshape(2, n_neg, half), neg_ids, panel_owner, total)
     return (mean_loss.reshape(()), event_grad, table_grad)

time: 107 us -> 104 us (0.972)
  Pallas kernels: 105 us -> 101 us
    pallas_call x1, Pallas kernels: 100 us -> 96.8 us  [per_device(): pl.pallas_call(functools.partial(main_kernel, n_seq, n_item), out_shape=(...]
where the time goes in v6:
time: 104 us; the launch traced here: 103 us
  Pallas kernels  101 us (97%)
  between operations  1.31 us (1%)
    pallas_call x1, Pallas kernels, per_device(): pl.pallas_call(functools.partial(main_kernel, n_seq, n_item), out_shape=(...  96.8 us
    pallas_call x1, Pallas kernels, per_device(): pl.pallas_call(functools.partial(scatter_kernel, n_item, scale), out_shap...  4.69 us

profile of v6, /device:TPU:1, one launch (start us, length us, event | category | flops | bytes accessed | tf_op | source)
XLA Modules:
  0.0 103.5 jit_solution(18139988508100005662)
XLA Ops:
  1.3 96.8 %main.1 = (f32[1,128,512]{2,1,0:T(8,128)}, f32[2,4,2,4,64,256]{5,4,3,2,1,0:T(8,128)}, f32[8,128]{1,0:T(8,128)}) custom-call(f32[1,128,512]{2,1,0:T(8,128)} %ev_ref.1, f32[512,2048]{1,0:T(8,128)} %w_ref.1, f32[1,512]{1,0:T(1,128)} %bitcast.6, f32[512,512]{1,0:T(8,128)} %wo_ref.1, f32[1024,512]{1,0:T(8,128)} %table_ref.1, s32[1,4]{1,0:T(1,128)} %lens_ref.1, ...), custom_call_target="tpu_custom_call" | custom-call | tf_op jit(solution)/shard_map/main/pallas_call | solution.py:801
  98.1 0.0 copy-start
  98.1 4.7 %scatter.1 = (f32[1024,512]{1,0:T(8,128)}, f32[1,1]{1,0:T(1,128)}) custom-call(f32[2,2048,256]{2,1,0:T(8,128)} %bitcast.4, s32[4,512]{1,0:T(4,128)} %neg_ref.3, s32[4]{0:T(128)} %owner_ref.1, f32[8,128]{1,0:T(8,128)} %get-tuple-element.9.total_ref), custom_call_target="tpu_custom_call" | custom-call | tf_op jit(solution)/shard_map/scatter/pallas_call | solution.py:822
  102.8 0.0 copy-done
  102.8 0.7 copy.15
Async XLA Ops:
  98.1 4.7 %copy-start = (f32[1,128,512]{2,1,0:T(8,128)S(1)}, f32[1,128,512]{2,1,0:T(8,128)}, u32[]{:S(2)}) copy-start(f32[1,128,512]{2,1,0:T(8,128)} %get-tuple-element.17) | copy-start | bytes 786436

commit v7 on v3

--- a/solution.py
+++ b/solution.py
@@ -545,63 +545,98 @@
     for n in range(2):
         qs[n] = project(xo, 4 + n)
         gates[n] = project(xo, n)
-    att[...] = jnp.zeros_like(att)
     neg.pass_x()
-    ev.forward()
 
     lane_head = lax.broadcasted_iota(jnp.int32, (tok, 128), 1) // hd
-    row = pc.s * tok + lax.broadcasted_iota(jnp.int32, (tok, step), 0)
-    lane = lax.broadcasted_iota(jnp.int32, (tok, step), 1)
-    begin = jnp.zeros((tok, step), jnp.int32)
+    sub = lax.broadcasted_iota(jnp.int32, (tok, tok), 0)
+    lane = lax.broadcasted_iota(jnp.int32, (tok, tok), 1)
+    row = pc.s * tok + sub
+    begin = jnp.zeros((tok, tok), jnp.int32)
     end = jnp.zeros((1, 1), jnp.int32)
     for u in range(lens_ref.shape[1]):
         end = end + lens_ref[0:1, u:u + 1]
         wide = jnp.broadcast_to(end, row.shape)
         begin = jnp.where(row >= wide, wide, begin)
 
-    def attend(y):
-        xs = split(jnp.concatenate([ev_all[2 * y], ev_all[2 * y + 1]], axis=0))
-
+    def stacked(m, lanes):
+        q = qs[m][:, lanes]
+        parts = [jnp.where(lane_head == h, q, 0.0) for h in range(hpg)]
+        return split(jnp.concatenate(parts, axis=0))
+
+    def collect(m, lanes, o, base):
+        got = base
+        for h in range(hpg):
+            got = got + jnp.where(lane_head == h, o[h * tok:(h + 1) * tok], 0.0)
+        att[m, :, lanes] = got
+
+    def weigh(sc, allow):
+        pr = (sc * sigmoid(sc)).reshape(hpg, tok, sc.shape[1]) * allow[None]
+        return split(pr.reshape(sc.shape))
+
+    def keys_values(xs, n_rows):
         def kv_step(n, _):
-            kvh[n], kvl[n] = split(project(xs, jnp.where(n < 2, 2 + n, 4 + n)))
+            hi, lo = split(project(xs, jnp.where(n < 2, 2 + n, 4 + n)))
+            kvh[n, :n_rows], kvl[n, :n_rows] = hi, lo
             return 0
 
         lax.fori_loop(0, 4, kv_step, 0)
-        col = y * step + lane
-        allow = jnp.where((col >= begin) & (col <= row), 1.0, 0.0)
+
+    def attend_own():
+        keys_values(xo, tok)
+        ev.forward()
+        allow = jnp.where((lane <= sub) & (pc.s * tok + lane >= begin), 1.0, 0.0)
+
+        def heads(m, _):
+            for g in range(half // 128):
+                lanes = slice(g * 128, (g + 1) * 128)
+                kh, kl = kvh[2 + m, :tok, lanes], kvl[2 + m, :tok, lanes]
+                vh, vl = kvh[m, :tok, lanes], kvl[m, :tok, lanes]
+                both = jnp.concatenate(stacked(m, lanes), axis=1)
+                kk = jnp.concatenate([kh, kh], axis=1)
+                k0 = jnp.concatenate([kl, jnp.zeros_like(kl)], axis=1)
+                sc = mm(both, jnp.concatenate([kk, k0], axis=0), NT)
+                pp = jnp.concatenate(weigh(sc[:, :tok] + sc[:, tok:], allow), axis=1)
+                vv = jnp.concatenate([vh, vl], axis=1)
+                o = mm(pp, jnp.concatenate([vv, vv], axis=0))
+                collect(m, lanes, o[:, :128] + o[:, 128:], jnp.zeros((tok, 128), f32))
+            return 0
+
+        lax.fori_loop(0, 2, heads, 0)
+
+    def attend(back, between):
+        blocks = [(pc.s + pc.S - back - d) % pc.S for d in (0, 1)]
+        keys_values(split(jnp.concatenate([ev_all[b] for b in blocks], axis=0)), step)
+        between()
+        cols = [b * tok + lane for b in blocks]
+        allow = [jnp.where((c >= begin) & (c <= row), 1.0, 0.0) for c in cols]
+        allow = jnp.concatenate(allow, axis=1)
 
         def heads(m, _):
             for g in range(half // 128):
                 lanes = slice(g * 128, (g + 1) * 128)
                 kh, kl = kvh[2 + m][:, lanes], kvl[2 + m][:, lanes]
                 vh, vl = kvh[m][:, lanes], kvl[m][:, lanes]
-                q = qs[m][:, lanes]
-                stack = [jnp.where(lane_head == h, q, 0.0) for h in range(hpg)]
-                qh, ql = split(jnp.concatenate(stack, axis=0))
+                qh, ql = stacked(m, lanes)
                 two = jnp.concatenate([qh, ql], axis=1)
                 sc = mm(two, jnp.concatenate([kh, kh], axis=1), NT) + mm(qh, kl, NT)
-                pr = (sc * sigmoid(sc)).reshape(hpg, tok, step) * allow[None]
-                ph, plo = split(pr.reshape(hpg * tok, step))
+                ph, plo = weigh(sc, allow)
                 o = mm(ph, jnp.concatenate([vh, vl], axis=1))
                 o = (o[:, :128] + o[:, 128:]) + mm(plo, vh)
-                got = att[m, :, lanes]
-                for h in range(hpg):
-                    got = got + jnp.where(lane_head == h, o[h * tok:(h + 1) * tok], 0.0)
-                att[m, :, lanes] = got
+                collect(m, lanes, o, att[m, :, lanes])
             return 0
 
         lax.fori_loop(0, 2, heads, 0)
 
-    ev.pair(0)
-    attend(pc.y)
+    attend_own()
     ev.near()
     neg.start_z()
+    ev.pair(0)
+    ev.pair(1)
+    attend(1, lambda: None)
     ev.far()
-    ev.pair(1)
-    attend(ev.ring.left)
     neg.start_gather()
     ev.pair(2)
-    attend(ev.ring.opp)
+    attend(3, lambda: None)
     neg.wait_z()
     spread.rx.start()
 
@@ -664,12 +699,14 @@
     mcol = jnp.broadcast_to(mine[tok:tok + 1, tok:tok + 1], (tok, step)).astype(jnp.int32)
     acc[...] = jnp.zeros_like(acc)
 
+    lane2 = lax.broadcasted_iota(jnp.int32, (tok, step), 1)
+
     def own_tokens(j):
         n0 = split(neg_all[0, j // 2, j % 2].reshape(share, half))
         n1 = split(neg_all[1, j // 2, j % 2].reshape(share, half))
         logits = mm3(oh[0], n0, NT) + mm3(oh[1], n1, NT)
-        live = (jnp.right_shift(mcol, 2 * j + lane // 128) & 1).astype(f32)
-        g, _, _ = loss_core(logits, lane + j * share == tcol, live)
+        live = (jnp.right_shift(mcol, 2 * j + lane2 // 128) & 1).astype(f32)
+        g, _, _ = loss_core(logits, lane2 + j * share == tcol, live)
         gs = split(g)
         acc[0] += mm3(gs, n0)
         acc[1] += mm3(gs, n1)
@@ -687,10 +724,10 @@
     spread.ry.forward()
     pan.start_z()
     loss.start_z()
+    pan.start_gather()
+    loss.start_s()
     spread.near()
     own_pair(1, spread.ry.left)
-    pan.start_gather()
-    loss.start_s()
     own_pair(2, spread.ry.right)
     pan.wait_z()
     steps = list(zip(lane_a.steps(), lane_b.steps()))
@@ -713,20 +750,25 @@
     item = lax.axis_index("item")
     rows = table_ref.shape[0]
     panel = neg_ref.shape[1]
-    half = buf.shape[2]
+    half = buf.shape[3]
+    def fetch(p):
+        return pltpu.make_async_copy(
+            panel_all.at[:, pl.ds(p * panel, panel), :], buf.at[p], sem.at[p]
+        )
+
+    for p in range(neg_ref.shape[0]):
+        pl.when(owner_ref[p] == item)(fetch(p).start)
     table_ref[...] = jnp.zeros_like(table_ref)
     loss_ref[0, 0] = jnp.max(total_ref[...]) * scale
     for p in range(neg_ref.shape[0]):
 
         @pl.when(owner_ref[p] == item)
         def _():
-            copy = pltpu.make_async_copy(panel_all.at[:, pl.ds(p * panel, panel), :], buf, sem)
-            copy.start()
             spot = lax.broadcasted_iota(jnp.int32, (rows, panel), 0)
             pick = jnp.where(spot == neg_ref[pl.ds(p, 1), :], 1.0, 0.0).astype(bf16)
-            copy.wait()
+            fetch(p).wait()
             for k in (0, 1):
-                hi, lo = split(buf[k])
+                hi, lo = split(buf[p, k])
                 table_ref[:, k * half:(k + 1) * half] += mm(pick, hi) + mm(pick, lo)
 
 
@@ -779,7 +821,7 @@
         functools.partial(scatter_kernel, n_item, scale),
         out_shape=(shape(item_table.shape, f32), shape((1, 1), f32)),
         in_specs=[ANY, VM, SM, VM], out_specs=(VM, SM),
-        scratch_shapes=[pltpu.VMEM((2, neg_ids.shape[1], half), f32), pltpu.SemaphoreType.DMA],
+        scratch_shapes=[pltpu.VMEM((neg_ids.shape[0], 2, neg_ids.shape[1], half), f32), dma(neg_ids.shape[0])],
         compiler_params=params(), name="scatter",
     )(panel_all.reshape(2, n_neg, half), neg_ids, panel_owner, total)
     return (mean_loss.reshape(()), event_grad, table_grad)

time: 97.4 us -> 95.1 us (0.976)
  Pallas kernels: 95.2 us -> 92.9 us
    pallas_call x1, Pallas kernels: 90.4 us -> 88.2 us  [per_device(): pl.pallas_call(functools.partial(main_kernel, n_seq, n_item), out_shape=(...]
where the time goes in v7:
time: 95.1 us; the launch traced here: 94.9 us
  Pallas kernels  92.9 us (98%)
  between operations  1.31 us (1%)
    pallas_call x1, Pallas kernels, per_device(): pl.pallas_call(functools.partial(main_kernel, n_seq, n_item), out_shape=(...  88.2 us
    pallas_call x1, Pallas kernels, per_device(): pl.pallas_call(functools.partial(scatter_kernel, n_item, scale), out_shap...  4.69 us

profile of v7, /device:TPU:1, one launch (start us, length us, event | category | flops | bytes accessed | tf_op | source)
XLA Modules:
  0.0 94.9 jit_solution(5323639505130548732)
XLA Ops:
  1.3 88.2 %main.1 = (f32[1,128,512]{2,1,0:T(8,128)}, f32[2,4,2,4,64,256]{5,4,3,2,1,0:T(8,128)}, f32[8,128]{1,0:T(8,128)}) custom-call(f32[1,128,512]{2,1,0:T(8,128)} %ev_ref.1, f32[512,2048]{1,0:T(8,128)} %w_ref.1, f32[1,512]{1,0:T(1,128)} %bitcast.6, f32[512,512]{1,0:T(8,128)} %wo_ref.1, f32[1024,512]{1,0:T(8,128)} %table_ref.1, s32[1,4]{1,0:T(1,128)} %lens_ref.1, ...), custom_call_target="tpu_custom_call" | custom-call | tf_op jit(solution)/shard_map/main/pallas_call | solution.py:799
  89.5 0.0 copy-start
  89.5 4.7 %scatter.1 = (f32[1024,512]{1,0:T(8,128)}, f32[1,1]{1,0:T(1,128)}) custom-call(f32[2,2048,256]{2,1,0:T(8,128)} %bitcast.4, s32[4,512]{1,0:T(4,128)} %neg_ref.3, s32[4]{0:T(128)} %owner_ref.1, f32[8,128]{1,0:T(8,128)} %get-tuple-element.9.total_ref), custom_call_target="tpu_custom_call" | custom-call | tf_op jit(solution)/shard_map/scatter/pallas_call | solution.py:820
  94.2 0.0 copy-done
  94.2 0.7 copy.15
Async XLA Ops:
  89.5 4.7 %copy-start = (f32[1,128,512]{2,1,0:T(8,128)S(1)}, f32[1,128,512]{2,1,0:T(8,128)}, u32[]{:S(2)}) copy-start(f32[1,128,512]{2,1,0:T(8,128)} %get-tuple-element.17) | copy-start | bytes 786436

commit v8 on v7

--- a/solution.py
+++ b/solution.py
@@ -628,13 +628,12 @@
         lax.fori_loop(0, 2, heads, 0)
 
     attend_own()
+    neg.start_z()
     ev.near()
-    neg.start_z()
     ev.pair(0)
     ev.pair(1)
-    attend(1, lambda: None)
+    attend(1, neg.start_gather)
     ev.far()
-    neg.start_gather()
     ev.pair(2)
     attend(3, lambda: None)
     neg.wait_z()

time: 95.1 us -> 95.4 us (level)
  no operation moved by 1% of the time
where the time goes in v8:
time: 95.4 us; the launch traced here: 95.2 us
  Pallas kernels  93.2 us (98%)
  between operations  1.31 us (1%)
    pallas_call x1, Pallas kernels, per_device(): pl.pallas_call(functools.partial(main_kernel, n_seq, n_item), out_shape=(...  88.5 us
    pallas_call x1, Pallas kernels, per_device(): pl.pallas_call(functools.partial(scatter_kernel, n_item, scale), out_shap...  4.69 us

profile of v8, /device:TPU:1, one launch (start us, length us, event | category | flops | bytes accessed | tf_op | source)
XLA Modules:
  0.0 95.2 jit_solution(5600743910802844116)
XLA Ops:
  1.3 88.5 %main.1 = (f32[1,128,512]{2,1,0:T(8,128)}, f32[2,4,2,4,64,256]{5,4,3,2,1,0:T(8,128)}, f32[8,128]{1,0:T(8,128)}) custom-call(f32[1,128,512]{2,1,0:T(8,128)} %ev_ref.1, f32[512,2048]{1,0:T(8,128)} %w_ref.1, f32[1,512]{1,0:T(1,128)} %bitcast.6, f32[512,512]{1,0:T(8,128)} %wo_ref.1, f32[1024,512]{1,0:T(8,128)} %table_ref.1, s32[1,4]{1,0:T(1,128)} %lens_ref.1, ...), custom_call_target="tpu_custom_call" | custom-call | tf_op jit(solution)/shard_map/main/pallas_call | solution.py:798
  89.8 0.0 copy-start
  89.8 4.7 %scatter.1 = (f32[1024,512]{1,0:T(8,128)}, f32[1,1]{1,0:T(1,128)}) custom-call(f32[2,2048,256]{2,1,0:T(8,128)} %bitcast.4, s32[4,512]{1,0:T(4,128)} %neg_ref.3, s32[4]{0:T(128)} %owner_ref.1, f32[8,128]{1,0:T(8,128)} %get-tuple-element.9.total_ref), custom_call_target="tpu_custom_call" | custom-call | tf_op jit(solution)/shard_map/scatter/pallas_call | solution.py:819
  94.5 0.0 copy-done
  94.5 0.7 copy.15
Async XLA Ops:
  89.8 4.7 %copy-start = (f32[1,128,512]{2,1,0:T(8,128)S(1)}, f32[1,128,512]{2,1,0:T(8,128)}, u32[]{:S(2)}) copy-start(f32[1,128,512]{2,1,0:T(8,128)} %get-tuple-element.17) | copy-start | bytes 786436
